TPU v7x, 32 devices: a whole 2x2x4 slice. The times are simulated.
32 devices in a mesh: wide: 16 (over z, x, core), narrow: 2 (over y).
Axes of the slice: x: 2, y: 2, z: 4, core: 2. Of those that a mesh axis runs over, the one named last changes fastest.
Arguments:
- plots: bfloat16 [32, 1024, 768], P('wide', 'narrow'), may hold values from -6 to 6
- plot_grid: int32 [32, 2], P('wide'), may hold values from 2 to 512, as said below
- query_weight: bfloat16 [768, 768], P('wide'), may hold values from -0.109375 to 0.109375
- key_weight: bfloat16 [768, 768], P('wide'), may hold values from -0.109375 to 0.109375
- value_weight: bfloat16 [768, 768], P('wide'), may hold values from -0.21875 to 0.21875
- out_weight: bfloat16 [768, 768], P('wide'), may hold values from -0.625 to 0.625
- gate_weight: bfloat16 [768, 2048], P('wide'), may hold values from -0.21875 to 0.21875
- up_weight: bfloat16 [768, 2048], P('wide'), may hold values from -0.21875 to 0.21875
- down_weight: bfloat16 [2048, 768], P('wide'), may hold values from -0.125 to 0.125
- gain_attn: bfloat16 [768], P('wide'), may hold values from 0.5 to 1.5
- gain_mlp: bfloat16 [768], P('wide'), may hold values from 0.5 to 1.5
- cotangent: bfloat16 [32, 1024, 768], P('wide', 'narrow'), may hold values from -6 to 6
Outputs:
- block_out: bfloat16 [32, 1024, 768], P('wide', 'narrow')
- grad_plots: bfloat16 [32, 1024, 768], P('wide', 'narrow')
- grad_query: float32 [768, 768], P('wide')
- grad_key: float32 [768, 768], P('wide')
- grad_value: float32 [768, 768], P('wide')
- grad_out: float32 [768, 768], P('wide')
- grad_gate: float32 [768, 2048], P('wide')
- grad_up: float32 [768, 2048], P('wide')
- grad_down: float32 [2048, 768], P('wide')
- grad_gain_attn: float32 [768], P('wide')
- grad_gain_mlp: float32 [768], P('wide')
Inputs may be any that keep to these rules, and one draw needn't show every extreme that they name: `plot_grid`: rows times columns of every plot is at most 1024 and equals it for some plot; rows are 2 to 32.
All inputs are finite; a program needn't handle non-finite values.
Results may differ from a plain program's by a relative error of at most 0.023.
Values may be sent and summed in bfloat16 or wider, within the bound.
A program may use at most 192 MiB of HBM per device.

v0:
```python
import jax
import jax.numpy as jnp
from jax import lax
from jax.sharding import PartitionSpec as P

HEADS = 12
HEAD_DIM = 64


epsilon = 1e-06


def norm_rows(values, gain):
    return values * lax.rsqrt(jnp.mean(values * values, axis=-1, keepdims=True) + epsilon) * gain


def gated(gate_pre, up_pre):
    return jax.nn.gelu(gate_pre, approximate=True) * up_pre


def to_heads(tensor):
    return tensor.reshape(tensor.shape[0], tensor.shape[1], HEADS, HEAD_DIM).transpose(2, 0, 1, 3)


def from_heads(tensor):
    return tensor.transpose(1, 2, 0, 3).reshape(tensor.shape[1], tensor.shape[2], HEADS * HEAD_DIM)


def masked_scores(query_one, keys_one, valid):
    scores = jnp.einsum("pqe,pke->pqk", query_one, keys_one, preferred_element_type=jnp.float32)
    return jnp.where(valid[:, None, :], scores, -1e30)


def weight_grad(left, right):
    return jnp.einsum("psd,pse->de", left, right, preferred_element_type=jnp.float32)


def back_product(grad_rows, weight):
    return jnp.einsum("pse,de->psd", grad_rows, weight, preferred_element_type=jnp.float32)


def forward_pass(inputs, weights, valid):
    (
        query_weight,
        key_weight,
        value_weight,
        out_weight,
        gate_weight,
        up_weight,
        down_weight,
        gain_attn,
        gain_mlp,
    ) = weights
    normed = norm_rows(inputs, gain_attn.astype(jnp.float32)).astype(jnp.bfloat16)
    query = jnp.dot(normed, query_weight, preferred_element_type=jnp.float32).astype(jnp.bfloat16)
    keys_local = jnp.dot(normed, key_weight, preferred_element_type=jnp.float32).astype(
        jnp.bfloat16
    )
    values_local = jnp.dot(normed, value_weight, preferred_element_type=jnp.float32).astype(
        jnp.bfloat16
    )
    keys_all, values_all = (
        lax.all_gather(keys_local, "narrow", axis=1, tiled=True),
        lax.all_gather(values_local, "narrow", axis=1, tiled=True),
    )
    query_heads = to_heads(query)
    key_heads = to_heads(keys_all)
    value_heads = to_heads(values_all)

    def head_forward(operands):
        query_one, keys_one, values_one = operands
        scores = masked_scores(query_one, keys_one, valid)
        row_max = jnp.max(scores, axis=-1, keepdims=True)
        exponent = jnp.exp(scores - row_max)
        total = jnp.sum(exponent, axis=-1, keepdims=True)
        mixed = jnp.einsum(
            "pqk,pke->pqe",
            (exponent / total).astype(jnp.bfloat16),
            values_one,
            preferred_element_type=jnp.float32,
        )
        return (mixed.astype(jnp.bfloat16), (row_max + jnp.log(total))[..., 0])

    mixed_heads, log_total = lax.map(head_forward, (query_heads, key_heads, value_heads))
    attended = from_heads(mixed_heads)
    hidden_in = inputs + jnp.dot(attended, out_weight, preferred_element_type=jnp.float32)
    normed_mlp = norm_rows(hidden_in, gain_mlp.astype(jnp.float32)).astype(jnp.bfloat16)
    gate_pre = jnp.dot(normed_mlp, gate_weight, preferred_element_type=jnp.float32)
    up_pre = jnp.dot(normed_mlp, up_weight, preferred_element_type=jnp.float32)
    activated = gated(gate_pre, up_pre).astype(jnp.bfloat16)
    output = hidden_in + jnp.dot(activated, down_weight, preferred_element_type=jnp.float32)
    saved = (
        normed,
        query_heads,
        key_heads,
        value_heads,
        log_total,
        attended,
        hidden_in,
        normed_mlp,
        gate_pre,
        up_pre,
        activated,
    )
    return (output, saved)


def body(
    plots,
    plot_grid,
    query_weight,
    key_weight,
    value_weight,
    out_weight,
    gate_weight,
    up_weight,
    down_weight,
    gain_attn,
    gain_mlp,
    cotangent,
):
    shards = (
        query_weight,
        key_weight,
        value_weight,
        out_weight,
        gate_weight,
        up_weight,
        down_weight,
        gain_attn,
        gain_mlp,
    )
    inputs = plots.astype(jnp.float32)
    counts = plot_grid[:, 0] * plot_grid[:, 1]
    length = plots.shape[1] * lax.axis_size("narrow")
    valid = jnp.arange(length)[None, :] < counts[:, None]
    weights = (
        lax.all_gather(shards[0], "wide", axis=0, tiled=True),
        lax.all_gather(shards[1], "wide", axis=0, tiled=True),
        lax.all_gather(shards[2], "wide", axis=0, tiled=True),
        lax.all_gather(shards[3], "wide", axis=0, tiled=True),
        lax.all_gather(shards[4], "wide", axis=0, tiled=True),
        lax.all_gather(shards[5], "wide", axis=0, tiled=True),
        lax.all_gather(shards[6], "wide", axis=0, tiled=True),
        lax.all_gather(shards[7], "wide", axis=0, tiled=True),
        lax.all_gather(shards[8], "wide", axis=0, tiled=True),
    )
    output, saved = forward_pass(inputs, weights, valid)
    weights = (
        lax.all_gather(shards[0], "wide", axis=0, tiled=True),
        lax.all_gather(shards[1], "wide", axis=0, tiled=True),
        lax.all_gather(shards[2], "wide", axis=0, tiled=True),
        lax.all_gather(shards[3], "wide", axis=0, tiled=True),
        lax.all_gather(shards[4], "wide", axis=0, tiled=True),
        lax.all_gather(shards[5], "wide", axis=0, tiled=True),
        lax.all_gather(shards[6], "wide", axis=0, tiled=True),
        lax.all_gather(shards[7], "wide", axis=0, tiled=True),
        lax.all_gather(shards[8], "wide", axis=0, tiled=True),
    )
    rerun, saved = forward_pass(inputs, weights, valid)
    (
        normed,
        query_heads,
        key_heads,
        value_heads,
        log_total,
        attended,
        hidden_in,
        normed_mlp,
        gate_pre,
        up_pre,
        activated,
    ) = saved
    (
        full_query,
        full_key,
        full_value,
        full_out,
        full_gate,
        full_up,
        full_down,
        full_gain_attn,
        full_gain_mlp,
    ) = weights
    grad_output = cotangent.astype(jnp.float32)
    grad_branch = grad_output.astype(jnp.bfloat16)
    grad_down = weight_grad(activated, grad_branch)
    grad_act = back_product(grad_branch, full_down)
    gate_value, gate_pull = jax.vjp(gated, gate_pre, up_pre)
    grad_gate_pre, grad_up_pre = gate_pull(grad_act)
    grad_gate_low = grad_gate_pre.astype(jnp.bfloat16)
    grad_up_low = grad_up_pre.astype(jnp.bfloat16)
    grad_gate = weight_grad(normed_mlp, grad_gate_low)
    grad_up = weight_grad(normed_mlp, grad_up_low)
    grad_normed_mlp = back_product(grad_gate_low, full_gate) + back_product(grad_up_low, full_up)
    norm_value, norm_pull = jax.vjp(norm_rows, hidden_in, full_gain_mlp.astype(jnp.float32))
    grad_hidden_norm, grad_gain_mlp = norm_pull(grad_normed_mlp)
    grad_hidden = grad_output + grad_hidden_norm
    grad_hidden_low = grad_hidden.astype(jnp.bfloat16)
    grad_out = weight_grad(attended, grad_hidden_low)
    grad_attended = back_product(grad_hidden_low, full_out).astype(jnp.bfloat16)
    grad_heads = to_heads(grad_attended)

    def head_backward(operands):
        query_one, keys_one, values_one, log_one, grad_one = operands
        scores = masked_scores(query_one, keys_one, valid)
        attention = jnp.exp(scores - log_one[..., None])
        grad_soft = jnp.einsum(
            "pqe,pke->pqk", grad_one, values_one, preferred_element_type=jnp.float32
        )
        row_dot = jnp.sum(attention * grad_soft, axis=-1, keepdims=True)
        grad_scores = (attention * (grad_soft - row_dot)).astype(jnp.bfloat16)
        grad_query_one = jnp.einsum(
            "pqk,pke->pqe", grad_scores, keys_one, preferred_element_type=jnp.float32
        )
        grad_keys_one = jnp.einsum(
            "pqk,pqe->pke", grad_scores, query_one, preferred_element_type=jnp.float32
        )
        grad_values_one = jnp.einsum(
            "pqk,pqe->pke",
            attention.astype(jnp.bfloat16),
            grad_one,
            preferred_element_type=jnp.float32,
        )
        return (grad_query_one, grad_keys_one, grad_values_one)

    grad_query_heads, grad_key_heads, grad_value_heads = lax.map(
        head_backward, (query_heads, key_heads, value_heads, log_total, grad_heads)
    )
    grad_key_local, grad_value_local = (
        lax.psum_scatter(
            grad_key_heads.astype(jnp.bfloat16), "narrow", scatter_dimension=2, tiled=True
        ).astype(jnp.float32),
        lax.psum_scatter(
            grad_value_heads.astype(jnp.bfloat16), "narrow", scatter_dimension=2, tiled=True
        ).astype(jnp.float32),
    )
    grad_query_low = from_heads(grad_query_heads).astype(jnp.bfloat16)
    grad_key_low = from_heads(grad_key_local).astype(jnp.bfloat16)
    grad_value_low = from_heads(grad_value_local).astype(jnp.bfloat16)
    grad_query = weight_grad(normed, grad_query_low)
    grad_key = weight_grad(normed, grad_key_low)
    grad_value = weight_grad(normed, grad_value_low)
    grad_normed = (
        back_product(grad_query_low, full_query)
        + back_product(grad_key_low, full_key)
        + back_product(grad_value_low, full_value)
    )
    first_value, first_pull = jax.vjp(norm_rows, inputs, full_gain_attn.astype(jnp.float32))
    grad_input_norm, grad_gain_attn = first_pull(grad_normed)
    grad_plots = (grad_hidden + grad_input_norm).astype(jnp.bfloat16)
    owned = (
        lax.psum_scatter(
            grad_query.astype(jnp.bfloat16), "wide", scatter_dimension=0, tiled=True
        ).astype(jnp.float32),
        lax.psum_scatter(
            grad_key.astype(jnp.bfloat16), "wide", scatter_dimension=0, tiled=True
        ).astype(jnp.float32),
        lax.psum_scatter(
            grad_value.astype(jnp.bfloat16), "wide", scatter_dimension=0, tiled=True
        ).astype(jnp.float32),
        lax.psum_scatter(
            grad_out.astype(jnp.bfloat16), "wide", scatter_dimension=0, tiled=True
        ).astype(jnp.float32),
        lax.psum_scatter(
            grad_gate.astype(jnp.bfloat16), "wide", scatter_dimension=0, tiled=True
        ).astype(jnp.float32),
        lax.psum_scatter(
            grad_up.astype(jnp.bfloat16), "wide", scatter_dimension=0, tiled=True
        ).astype(jnp.float32),
        lax.psum_scatter(
            grad_down.astype(jnp.bfloat16), "wide", scatter_dimension=0, tiled=True
        ).astype(jnp.float32),
        lax.psum_scatter(
            grad_gain_attn.astype(jnp.bfloat16), "wide", scatter_dimension=0, tiled=True
        ).astype(jnp.float32),
        lax.psum_scatter(
            grad_gain_mlp.astype(jnp.bfloat16), "wide", scatter_dimension=0, tiled=True
        ).astype(jnp.float32),
    )
    summed = (
        lax.psum(owned[0].astype(jnp.bfloat16), "narrow").astype(jnp.float32),
        lax.psum(owned[1].astype(jnp.bfloat16), "narrow").astype(jnp.float32),
        lax.psum(owned[2].astype(jnp.bfloat16), "narrow").astype(jnp.float32),
        lax.psum(owned[3].astype(jnp.bfloat16), "narrow").astype(jnp.float32),
        lax.psum(owned[4].astype(jnp.bfloat16), "narrow").astype(jnp.float32),
        lax.psum(owned[5].astype(jnp.bfloat16), "narrow").astype(jnp.float32),
        lax.psum(owned[6].astype(jnp.bfloat16), "narrow").astype(jnp.float32),
        lax.psum(owned[7].astype(jnp.bfloat16), "narrow").astype(jnp.float32),
        lax.psum(owned[8].astype(jnp.bfloat16), "narrow").astype(jnp.float32),
    )
    return (
        output.astype(jnp.bfloat16),
        grad_plots,
        summed[0],
        summed[1],
        summed[2],
        summed[3],
        summed[4],
        summed[5],
        summed[6],
        summed[7],
        summed[8],
    )


def solution(mesh):
    return jax.shard_map(
        body,
        mesh=mesh,
        in_specs=(
            P("wide", "narrow", None),
            P("wide", None),
            P("wide", None),
            P("wide", None),
            P("wide", None),
            P("wide", None),
            P("wide", None),
            P("wide", None),
            P("wide", None),
            P("wide"),
            P("wide"),
            P("wide", "narrow", None),
        ),
        out_specs=(
            P("wide", "narrow", None),
            P("wide", "narrow", None),
            P("wide", None),
            P("wide", None),
            P("wide", None),
            P("wide", None),
            P("wide", None),
            P("wide", None),
            P("wide", None),
            P("wide"),
            P("wide"),
        ),
        check_vma=False,
    )
```

profile of v0, /device:TPU:0, one launch (start us, length us, event | category | flops | bytes accessed | tf_op | source)
XLA Modules:
  0.0 1180.6 jit_solution(11535697762387463714)
XLA Ops:
  13.1 35.2 %all-reduce.5 = (bf16[768]{0:T(1024)(128)(2,1)S(1)}, bf16[768]{0:T(1024)(128)(2,1)S(1)}) all-reduce(bf16[768]{0:T(1024)(128)(2,1)S(1)} %dynamic-update-slice, bf16[768]{0:T(1024)(128)(2,1)S(1)} %dynamic-update-slice.1), channel_id=1, replica_groups=mesh['wide'=16,'narrow'=2] {'wide'}, use_global_device_ids=true, to_apply=%add | all-reduce | flops 1536 | bytes 6144
  55.9 35.2 %all-gather.16.cloned.1.call-done = bf16[768,768]{1,0:T(8,128)(2,1)} async-done(((bf16[48,768]{1,0:T(8,128)(2,1)}), bf16[768,768]{1,0:T(8,128)(2,1)}) %all-gather.16.cloned.1.call-update) | async-done | bytes 1179664 | tf_op jit(solution)/shard_map/all_gather | solution.py:140
  98.1 32.6 %all-gather.10.cloned.1.call-done = bf16[768,768]{1,0:T(8,128)(2,1)} async-done(((bf16[48,768]{1,0:T(8,128)(2,1)}), bf16[768,768]{1,0:T(8,128)(2,1)}) %all-gather.10.cloned.1.call-update) | async-done | bytes 1179664 | tf_op jit(solution)/shard_map/all_gather | solution.py:138
  136.0 40.7 %all-gather.14.cloned.1.call-done = bf16[2,1024,768]{2,1,0:T(8,128)(2,1)} async-done(((bf16[2,512,768]{2,1,0:T(8,128)(2,1)}), bf16[2,1024,768]{2,1,0:T(8,128)(2,1)}) %all-gather.14.cloned.1.call-update) | async-done | bytes 3145744 | tf_op jit(solution)/shard_map/all_gather | solution.py:63
  183.7 39.3 %all-gather.18.cloned.1.call-done = bf16[2,1024,768]{2,1,0:T(8,128)(2,1)} async-done(((bf16[2,512,768]{2,1,0:T(8,128)(2,1)}), bf16[2,1024,768]{2,1,0:T(8,128)(2,1)}) %all-gather.18.cloned.1.call-update) | async-done | bytes 3145744 | tf_op jit(solution)/shard_map/all_gather | solution.py:64
  233.0 66.4 %while.40 = (s32[]{:T(128)}, bf16[12,2,512,64]{2,3,0,1:T(8,128)(2,1)}, f32[12,2,512]{2,1,0:T(2,128)S(1)}, bf16[12,2,512,64]{2,3,1,0:T(8,128)(2,1)}, bf16[12,2,10...) while((s32[]{:T(128)}, ...), condition=%wide.region_9.10_spmd.clone, body=%wide.region_6.9_spmd.clone.sunk | while | flops 277939200 | bytes 13414505 | solution.py:84
  310.4 9.0 fusion.128
  319.4 37.3 %all-gather.26.cloned.1.call-done = bf16[2048,768]{1,0:T(8,128)(2,1)} async-done(((bf16[128,768]{1,0:T(8,128)(2,1)}), bf16[2048,768]{1,0:T(8,128)(2,1)}) %all-gather.26.cloned.1.call-update) | async-done | bytes 3145744 | tf_op jit(solution)/shard_map/all_gather | solution.py:144
  356.7 9.0 fusion.122
  365.7 37.3 %all-gather.22.cloned.1.call-done = bf16[768,2048]{1,0:T(8,128)(2,1)} async-done(((bf16[48,2048]{1,0:T(8,128)(2,1)}), bf16[768,2048]{1,0:T(8,128)(2,1)}) %all-gather.22.cloned.1.call-update) | async-done | bytes 3145744 | tf_op jit(solution)/shard_map/all_gather | solution.py:142
  403.0 16.6 %fusion.102 = (bf16[2,512,2048]{2,1,0:T(8,128)(2,1)S(1)}, bf16[2,512,2048]{2,1,0:T(8,128)(2,1)S(1)}, f32[2,512,2048]{2,1,0:T(8,128)}) fusion(f32[2,512,2048]{2,1,0:T(8,128)} %fusion.122, f32[2,512,2048]{2,1,0:T(8,128)} %fusion.128, bf16[2,512,768]{2,1,0:T(8,128)(2,1)} %multiply_convert_fusion.6, bf16[768,2048]{1,0:T(8,128)(2,1)} %all-gather.22.cloned.1.call-done), kind=kOutput, calls=%fused_computation.98 | convolution fusion | flops 3271557120 | bytes 38273024 | tf_op jit(solution)/shard_map/dot_general | solution.py:88
  419.6 5.1 fusion.126
  426.5 6.5 multiply_reduce_fusion.1
  440.7 135.4 %while.41 = (s32[]{:T(128)}, bf16[12,2,512,64]{2,3,0,1:T(8,128)(2,1)}, bf16[12,2,1024,64]{2,3,0,1:T(8,128)(2,1)}, bf16[12,2,1024,64]{2,3,0,1:T(8,128)(2,1)}, bf1...) while((s32[]{:T(128)}, ...), condition=%wide.region_14.15_spmd.clone, body=%wide.region_12.14_spmd.clone.sunk | while | flops 683672576 | bytes 34120832 | solution.py:227
  577.0 4.8 bitcast_convert_fusion.3
  586.6 7.8 bitcast_convert_fusion.1
  595.0 7.8 bitcast_convert_fusion.2
  603.5 13.2 %bitcast_convert_fusion = bf16[2048,768]{1,0:T(8,128)(2,1)} fusion(bf16[2,512,768]{2,1,0:T(8,128)(2,1)} %param.29, f32[2,512,2048]{2,1,0:T(8,128)} %fusion.128, f32[2,512,2048]{2,1,0:T(8,128)} %get-tuple-element.319), kind=kOutput, calls=%fused_computation.117 | convolution fusion | flops 3243769856 | bytes 21495808 | tf_op jit(solution)/shard_map/psd,pse->de/dot_general | solution.py:35
  618.2 96.5 %while.39 = (s32[]{:T(128)}, bf16[12,2,512,64]{2,3,0,1:T(8,128)(2,1)}, bf16[12,2,512,64]{2,3,1,0:T(8,128)(2,1)}, bf16[12,2,1024,64]{2,3,1,0:T(8,128)(2,1)S(1)}, ...) while((s32[]{:T(128)}, bf16[12,2,512,64]{2,3,0,1:T(8,128)(2,1)}, ...), condition=%wide.region_4.5_spmd.clone, body=%wide.region_1.4_spmd.clone.sunk | while | flops 273746944 | bytes 9191517 | solution.py:84
  726.8 5.7 fusion.135
  736.8 13.4 %add_convert_fusion = bf16[2,512,768]{2,1,0:T(8,128)(2,1)} fusion(f32[2,512,768]{2,1,0:T(8,128)} %copy-done.22, bf16[2048,768]{1,0:T(8,128)(2,1)} %all-gather.26.cloned.1.call-done, f32[2,512,2048]{2,1,0:T(8,128)} %fusion.135, bf16[768,2048]{1,0:T(8,128)(2,1)} %all-gather.24.cloned.1.call-done, f32[768]{0:T(1024)S(1)} %convert_element_type.190, ...), kind=kOutput, calls=%fused_computation.152 | convolution fusion | flops 6467354624 | bytes 19405824 | tf_op jit(solution)/shard_map/dot_general | solution.py:91
  750.2 5.0 fusion.152
  755.2 31.3 %reduce-scatter.14.cloned.1.call-done = bf16[48,768]{1,0:T(8,128)(2,1)} async-done(((bf16[768,768]{1,0:T(8,128)(2,1)}), bf16[48,768]{1,0:T(8,128)(2,1)}) %reduce-scatter.14.cloned.1.call-update) | async-done | bytes 73744 | tf_op jit(solution)/shard_map/reduce_scatter | solution.py:253
  786.6 69.0 %reduce-scatter.24.cloned.1.call-done = bf16[48,2048]{1,0:T(8,128)(2,1)} async-done(((bf16[768,2048]{1,0:T(8,128)(2,1)}), bf16[48,2048]{1,0:T(8,128)(2,1)}) %reduce-scatter.24.cloned.1.call-update) | async-done | bytes 196624 | tf_op jit(solution)/shard_map/reduce_scatter | solution.py:268
  855.5 68.8 %reduce-scatter.22.cloned.1.call-done = bf16[48,2048]{1,0:T(8,128)(2,1)} async-done(((bf16[768,2048]{1,0:T(8,128)(2,1)}), bf16[48,2048]{1,0:T(8,128)(2,1)}) %reduce-scatter.22.cloned.1.call-update) | async-done | bytes 196624 | tf_op jit(solution)/shard_map/reduce_scatter | solution.py:265
  924.4 68.9 %reduce-scatter.26.cloned.1.call-done = bf16[128,768]{1,0:T(8,128)(2,1)} async-done(((bf16[2048,768]{1,0:T(8,128)(2,1)}), bf16[128,768]{1,0:T(8,128)(2,1)}) %reduce-scatter.26.cloned.1.call-update) | async-done | bytes 196624 | tf_op jit(solution)/shard_map/reduce_scatter | solution.py:271
  993.3 60.5 %reduce-scatter.16.cloned.1.call-done = bf16[48,768]{1,0:T(8,128)(2,1)} async-done(((bf16[768,768]{1,0:T(8,128)(2,1)}), bf16[48,768]{1,0:T(8,128)(2,1)}) %reduce-scatter.16.cloned.1.call-update) | async-done | bytes 73744 | tf_op jit(solution)/shard_map/reduce_scatter | solution.py:256
  1053.8 61.2 %reduce-scatter.18.cloned.1.call-done = bf16[48,768]{1,0:T(8,128)(2,1)} async-done(((bf16[768,768]{1,0:T(8,128)(2,1)}), bf16[48,768]{1,0:T(8,128)(2,1)}) %reduce-scatter.18.cloned.1.call-update) | async-done | bytes 73744 | tf_op jit(solution)/shard_map/reduce_scatter | solution.py:259
  1115.0 6.9 fusion.116
  1122.0 29.6 %all-reduce.4 = (bf16[768]{0:T(1024)(128)(2,1)S(1)}, bf16[768]{0:T(1024)(128)(2,1)S(1)}) all-reduce(bf16[768]{0:T(1024)(128)(2,1)S(1)} %get-tuple-element.244, bf16[768]{0:T(1024)(128)(2,1)S(1)} %copy-done.15), channel_id=11, replica_groups=mesh['wide'=16,'narrow'=2] {'wide'}, use_global_device_ids=true, to_apply=%region_33.34.clone | all-reduce | flops 1536 | bytes 6144
  1151.8 4.9 all-reduce.6
  1157.7 4.8 fusion.119
  (337 shorter events, 396.5 us)
Async XLA Ops:
  7.2 44.3 %all-gather.12.cloned.1.call-start = ((), (), s32[]{:S(2)}) async-start(), calls=%async_computation.10 | async-start | bytes 1253376 | tf_op jit(solution)/shard_map/all_gather | solution.py:139
  7.9 83.2 %all-gather.16.cloned.1.call-start = ((), (), s32[]{:S(2)}) async-start(), calls=%async_computation.12 | async-start | bytes 1253376 | tf_op jit(solution)/shard_map/all_gather | solution.py:140
  8.7 122.1 %all-gather.10.cloned.1.call-start = ((), (), s32[]{:S(2)}) async-start(), calls=%async_computation.9 | async-start | bytes 1253376 | tf_op jit(solution)/shard_map/all_gather | solution.py:138
  9.4 167.2 %all-gather.14.cloned.1.call-start = ((), (), s32[]{:S(2)}) async-start(), calls=%async_computation.11 | async-start | bytes 4718592 | tf_op jit(solution)/shard_map/all_gather | solution.py:63
  48.3 82.4 %copy-start.8 = (f32[768]{0:T(1024)}, f32[768]{0:T(1024)S(1)}, u32[]{:S(2)}) copy-start(f32[768]{0:T(1024)S(1)} %convert_element_type.185) | copy-start | bytes 9220
  50.7 80.0 %copy-start.10 = (f32[2,512]{1,0:T(2,128)}, f32[2,512]{1,0:T(2,128)S(1)}, u32[]{:S(2)}) copy-start(f32[2,512]{1,0:T(2,128)S(1)} %fusion.160) | copy-start | bytes 12292
  50.7 40.4 %copy-start = (bf16[2,512,768]{2,1,0:T(8,128)(2,1)S(1)}, bf16[2,512,768]{2,1,0:T(8,128)(2,1)}, u32[]{:S(2)}) copy-start(bf16[2,512,768]{2,1,0:T(8,128)(2,1)} %param.18) | copy-start | bytes 4718596
  55.9 42.1 %copy-start.14 = (s32[2,2]{1,0:T(2,128)S(1)}, s32[2,2]{1,0:T(2,128)}, u32[]{:S(2)}) copy-start(s32[2,2]{1,0:T(2,128)} %param.19) | copy-start | bytes 52
  55.9 167.1 %all-gather.18.cloned.1.call-start = ((), (), s32[]{:S(2)}) async-start(), calls=%async_computation.13 | async-start | bytes 4718592 | tf_op jit(solution)/shard_map/all_gather | solution.py:64
  95.0 204.4 %all-gather.20.cloned.1.call-start = ((), (), s32[]{:S(2)}) async-start(), calls=%async_computation.14 | async-start | bytes 1253376 | tf_op jit(solution)/shard_map/all_gather | solution.py:141
  95.6 214.7 %all-gather.24.cloned.1.call-start = ((), (), s32[]{:S(2)}) async-start(), calls=%async_computation.16 | async-start | bytes 3342336 | tf_op jit(solution)/shard_map/all_gather | solution.py:143
  96.4 260.3 %all-gather.26.cloned.1.call-start = ((), (), s32[]{:S(2)}) async-start(), calls=%async_computation.17 | async-start | bytes 3342336 | tf_op jit(solution)/shard_map/all_gather | solution.py:144
  97.1 305.9 %all-gather.22.cloned.1.call-start = ((), (), s32[]{:S(2)}) async-start(), calls=%async_computation.15 | async-start | bytes 3342336 | tf_op jit(solution)/shard_map/all_gather | solution.py:142
  97.9 616.9 %reduce-scatter.10.cloned.1.call-start = ((), (), s32[]{:S(2)}) async-start(), calls=%async_computation.18 | async-start | bytes 4718592 | tf_op jit(solution)/shard_map/reduce_scatter | solution.py:231
  403.0 16.6 %copy-start.16 = (bf16[768,2048]{1,0:T(8,128)(2,1)S(1)}, bf16[768,2048]{1,0:T(8,128)(2,1)}, u32[]{:S(2)}) copy-start(bf16[768,2048]{1,0:T(8,128)(2,1)} %all-gather.24.cloned.1.call-done) | copy-start | bytes 9437188
  419.6 5.2 copy-start.24
  419.6 5.7 copy-start.23
  419.6 5.7 copy-start.4
  419.6 6.9 copy-start.17
  426.5 6.6 copy-start.6
  576.1 156.3 %reduce-scatter.12.cloned.1.call-start = ((), (), s32[]{:S(2)}) async-start(), calls=%async_computation.19 | async-start | bytes 4718592 | tf_op jit(solution)/shard_map/reduce_scatter | solution.py:234
  576.9 178.3 %reduce-scatter.20.cloned.1.call-start = ((), (), s32[]{:S(2)}) async-start(), calls=%async_computation.23 | async-start | bytes 1253376 | tf_op jit(solution)/shard_map/reduce_scatter | solution.py:262
  581.8 204.8 %reduce-scatter.14.cloned.1.call-start = ((), (), s32[]{:S(2)}) async-start(), calls=%async_computation.20 | async-start | bytes 1253376 | tf_op jit(solution)/shard_map/reduce_scatter | solution.py:253
  586.6 268.9 %reduce-scatter.24.cloned.1.call-start = ((), (), s32[]{:S(2)}) async-start(), calls=%async_computation.25 | async-start | bytes 3342336 | tf_op jit(solution)/shard_map/reduce_scatter | solution.py:268
  594.5 329.9 %reduce-scatter.22.cloned.1.call-start = ((), (), s32[]{:S(2)}) async-start(), calls=%async_computation.24 | async-start | bytes 3342336 | tf_op jit(solution)/shard_map/reduce_scatter | solution.py:265
  602.8 390.5 %reduce-scatter.26.cloned.1.call-start = ((), (), s32[]{:S(2)}) async-start(), calls=%async_computation.26 | async-start | bytes 3342336 | tf_op jit(solution)/shard_map/reduce_scatter | solution.py:271
  616.7 437.1 %reduce-scatter.16.cloned.1.call-start = ((), (), s32[]{:S(2)}) async-start(), calls=%async_computation.21 | async-start | bytes 1253376 | tf_op jit(solution)/shard_map/reduce_scatter | solution.py:256
  719.5 395.5 %reduce-scatter.18.cloned.1.call-start = ((), (), s32[]{:S(2)}) async-start(), calls=%async_computation.22 | async-start | bytes 1253376 | tf_op jit(solution)/shard_map/reduce_scatter | solution.py:259
  736.6 426.0 %all-reduce.10.cloned.1.call-start = ((), (), s32[]{:S(2)}) async-start(), calls=%async_computation.27 | async-start | bytes 1769472 | tf_op jit(solution)/shard_map/psum | solution.py:282
  750.2 364.8 %copy-start.7 = (bf16[12,2,512,64]{2,3,0,1:T(8,128)(2,1)S(1)}, bf16[12,2,512,64]{2,3,0,1:T(8,128)(2,1)}, u32[]{:S(2)}) copy-start(bf16[12,2,512,64]{2,3,0,1:T(8,128)(2,1)} %reduce-scatter.12.cloned.1.call-done) | copy-start | bytes 4718596
  1115.0 7.0 copy-start.15
  1115.0 42.7 %copy-start.13 = (f32[2,512]{1,0:T(2,128)S(1)}, f32[2,512]{1,0:T(2,128)}, u32[]{:S(2)}) copy-start(f32[2,512]{1,0:T(2,128)} %copy-done.12) | copy-start | bytes 12292
  (12 other events, 39.3 us)
Sparse Core Ops, SparseCore 0:
  10.3 41.1 all-gather.11
  53.8 37.3 all-gather.15
  93.4 37.2 all-gather.9
  132.7 43.8 all-gather.13
  178.0 44.9 all-gather.17
  225.1 38.3 all-gather.19
  265.8 44.4 all-gather.23
  312.6 43.9 all-gather.25
  359.0 43.9 all-gather.21
  576.3 42.1 reduce-scatter.9
  620.8 43.3 reduce-scatter.11
  667.7 57.9 reduce-scatter.19
  729.3 57.1 reduce-scatter.13
  790.2 65.2 reduce-scatter.23
  859.2 65.1 reduce-scatter.21
  928.0 65.2 reduce-scatter.25
  996.7 57.0 reduce-scatter.15
  1057.9 57.0 reduce-scatter.17
  1117.7 36.5 all-reduce.9
where the time goes:
time: 1190 us; the launch traced here: 1180 us
  waiting for transfers between devices  592 us (50%)
  matrix products  418 us (35%)
  blocking collectives  69.7 us (6%)
  other arithmetic  49 us (4%)
  local copies, waits for them, and re-layouts  33.3 us (3%)
  between operations  15.9 us (1%)
    dot_general x24, matrix products, head_forward(): jnp.einsum('pqk,pke->pqe', (exponent / total).astype(jnp.bfloat16), value...  78.1 us
    reduce_scatter x1, waiting for transfers between devices, body(): lax.psum_scatter(grad_up.astype(jnp.bfloat16), 'wide', scatter_dimension=...  69 us
    reduce_scatter x1, waiting for transfers between devices, body(): lax.psum_scatter(grad_down.astype(jnp.bfloat16), 'wide', scatter_dimensio...  68.9 us
    reduce_scatter x1, waiting for transfers between devices, body(): lax.psum_scatter(grad_gate.astype(jnp.bfloat16), 'wide', scatter_dimensio...  68.8 us
    unnamed x2, blocking collectives  64.8 us
    reduce_scatter x1, waiting for transfers between devices, body(): lax.psum_scatter(grad_value.astype(jnp.bfloat16), 'wide', scatter_dimensi...  61.2 us
    reduce_scatter x1, waiting for transfers between devices, body(): lax.psum_scatter(grad_key.astype(jnp.bfloat16), 'wide', scatter_dimension...  60.5 us
    sub x12, matrix products, head_forward(): exponent = jnp.exp(scores - row_max)  50.5 us
  transfers between devices with their start and end apart: 19, of which 14 were waited for; matrix products, arithmetic and copies ran while one was open for 27% of the time, Pallas kernels for 0%

commit v1 on v0

--- a/solution.py
+++ b/solution.py
@@ -1,6 +1,10 @@
+import functools
+
 import jax
 import jax.numpy as jnp
 from jax import lax
+from jax.experimental import pallas as pl
+from jax.experimental.pallas import tpu as pltpu
 from jax.sharding import PartitionSpec as P
 
 HEADS = 12
@@ -105,7 +109,7 @@
     return (output, saved)
 
 
-def body(
+def body_general(
     plots,
     plot_grid,
     query_weight,
@@ -304,9 +308,350 @@
     )
 
 
+F32, BF16 = jnp.float32, jnp.bfloat16
+ROOT = 0.7978845608028654
+CUBE = 0.044715
+VMEM_BYTES = 60 << 20
+
+
+def nn(left, right):
+    return lax.dot_general(left, right, (((1,), (0,)), ((), ())), preferred_element_type=F32)
+
+
+def nt(left, right):
+    return lax.dot_general(left, right, (((1,), (1,)), ((), ())), preferred_element_type=F32)
+
+
+def lanes_of(rows, width=128):
+    return lax.broadcasted_iota(jnp.int32, (rows, width), 1)
+
+
+def row_block(index, size):
+    return pl.ds(pl.multiple_of(index * size, size), size)
+
+
+def head_masks(pair, lane, flag):
+    first = jnp.where(lane < 64, pair, jnp.where(lane == 64, flag, 0.0))
+    second = jnp.where(lane >= 64, pair, jnp.where(lane == 0, flag, 0.0))
+    return first.astype(BF16), second.astype(BF16)
+
+
+def attend_forward(count_ref, x_ref, gain_ref, wq_ref, wk_ref, wv_ref, wo_ref,
+                   q_ref, k_ref, v_ref, normed_ref, mixed_ref, lse_ref, hidden_ref,
+                   qh, kh, vh, lse_cols):
+    slots = x_ref.shape[0]
+    tile = 256
+    tiles = slots // tile
+    pairs = HEADS // 2
+
+    def project(t, carry):
+        rows = row_block(t, tile)
+        x = x_ref[rows, :].astype(F32)
+        r = lax.rsqrt(jnp.mean(x * x, axis=-1, keepdims=True) + epsilon)
+        normed = (x * r * gain_ref[...]).astype(BF16)
+        normed_ref[rows, :] = normed
+        q_ref[rows, :] = nn(normed, wq_ref[...]).astype(BF16)
+        k_ref[rows, :] = nn(normed, wk_ref[...]).astype(BF16)
+        v_ref[rows, :] = nn(normed, wv_ref[...]).astype(BF16)
+        return carry
+
+    lax.fori_loop(0, tiles, project, 0)
+    count = count_ref[0]
+    lane = lanes_of(slots)
+    slot = lax.broadcasted_iota(jnp.int32, (slots, 128), 0)
+    bias = jnp.where(slot < count, 0.0, -1e30)
+    lse_cols[...] = jnp.zeros_like(lse_cols)
+    for h in range(2):
+        vh[h, :, 128:] = jnp.ones((slots, 128), BF16)
+
+    def pair_step(p, carry):
+        cols = row_block(p, 128)
+        kh[0], kh[1] = head_masks(k_ref[:, cols].astype(F32), lane, bias)
+        qp = q_ref[:, cols].astype(F32)
+        qh[0] = jnp.where(lane == 64, 1.0, qp).astype(BF16)
+        qh[1] = jnp.where(lane == 0, 1.0, qp).astype(BF16)
+        vh[0, :, :128], vh[1, :, :128] = head_masks(v_ref[:, cols].astype(F32), lane, 0.0)
+
+        def tile_step(t, carry):
+            rows = row_block(t, tile)
+            total = None
+            cols_out = lse_cols[rows, :]
+            for h in range(2):
+                score = nt(qh[h, rows, :], kh[h])
+                top = jnp.max(score, axis=1, keepdims=True)
+                weight = jnp.exp(score - top).astype(BF16)
+                acc = nn(weight, vh[h])
+                part = acc[:, :128] / acc[:, 128:]
+                total = part if total is None else total + part
+                cols_out = jnp.where(lanes_of(tile) == 2 * p + h, top + jnp.log(acc[:, 128:]), cols_out)
+            mixed_ref[rows, cols] = total.astype(BF16)
+            lse_cols[rows, :] = cols_out
+            return carry
+
+        lax.fori_loop(0, tiles, tile_step, 0)
+        return carry
+
+    lax.fori_loop(0, pairs, pair_step, 0)
+
+    def project_out(t, carry):
+        rows = row_block(t, tile)
+        hidden_ref[rows, :] = x_ref[rows, :].astype(F32) + nn(mixed_ref[rows, :], wo_ref[...])
+        lse_ref[:, rows] = jnp.transpose(lse_cols[rows, :])
+        return carry
+
+    lax.fori_loop(0, tiles, project_out, 0)
+
+
+def permuted_store(target, index, value, block):
+    blocks = target.shape[0] // block
+    deep = blocks // 4
+    turned = jnp.transpose(value)
+    for w in range(blocks):
+        z, x, c = w // 4, (w // 2) % 2, w % 2
+        place = (c * 2 + x) * deep + z
+        target[place * block:(place + 1) * block, index] = turned[w * block:(w + 1) * block, :]
+
+
+def mlp_both(hidden_ref, cot_ref, gain_ref, wg_ref, wu_ref, wd_ref,
+             out_ref, dhid_ref, gdown_ref, ggate_ref, gup_ref, ggain_ref,
+             nmt, actt, dg_s, du_s):
+    slots, d = hidden_ref.shape
+    ff = wg_ref.shape[1]
+    tile = 128
+    blocks = 16
+    ggain_ref[...] = jnp.zeros_like(ggain_ref)
+
+    def step(t, carry):
+        rows = row_block(t, tile)
+        hidden = hidden_ref[rows, :]
+        r = lax.rsqrt(jnp.mean(hidden * hidden, axis=-1, keepdims=True) + epsilon)
+        gain = gain_ref[...]
+        normed = (hidden * r * gain).astype(BF16)
+        permuted_store(nmt, rows, normed, d // blocks)
+        gate_pre = nn(normed, wg_ref[...])
+        up_pre = nn(normed, wu_ref[...])
+        square = gate_pre * gate_pre
+        inner = ROOT * gate_pre * (1.0 + CUBE * square)
+        th = jnp.tanh(inner)
+        half = 0.5 * (1.0 + th)
+        gelu = gate_pre * half
+        slope = half + 0.5 * gate_pre * (1.0 - th * th) * (ROOT * (1.0 + 3.0 * CUBE * square))
+        act = (gelu * up_pre).astype(BF16)
+        permuted_store(actt, rows, act, ff // blocks)
+        out_ref[rows, :] = (hidden + nn(act, wd_ref[...])).astype(BF16)
+        dy = cot_ref[rows, :]
+        d_act = nt(dy, wd_ref[...])
+        dg = (d_act * up_pre * slope).astype(BF16)
+        du = (d_act * gelu).astype(BF16)
+        dg_s[rows, :] = dg
+        du_s[rows, :] = du
+        dn = nt(dg, wg_ref[...]) + nt(du, wu_ref[...])
+        scaled = dn * gain
+        mean = jnp.mean(scaled * hidden, axis=-1, keepdims=True)
+        dhid_ref[rows, :] = dy.astype(F32) + r * scaled - hidden * (r * r * r * mean)
+        ggain_ref[...] += jnp.sum(dn * hidden * r, axis=0, keepdims=True)
+        return carry
+
+    lax.fori_loop(0, slots // tile, step, 0)
+
+    def down_step(n, carry):
+        cols = row_block(n, 128)
+        gdown_ref[:, cols] = nn(actt[...], cot_ref[:, cols]).astype(BF16)
+        return carry
+
+    lax.fori_loop(0, d // 128, down_step, 0)
+
+    def gate_step(n, carry):
+        cols = row_block(n, 256)
+        ggate_ref[:, cols] = nn(nmt[...], dg_s[:, cols]).astype(BF16)
+        gup_ref[:, cols] = nn(nmt[...], du_s[:, cols]).astype(BF16)
+        return carry
+
+    lax.fori_loop(0, ff // 256, gate_step, 0)
+
+
+def attend_backward(count_ref, x_ref, gain_ref, wq_ref, wk_ref, wv_ref, wo_ref,
+                    q_ref, k_ref, v_ref, normed_ref, mixed_ref, lse_ref, dhid_ref,
+                    gplots_ref, gq_ref, gk_ref, gv_ref, gout_ref, ggain_ref,
+                    dhl, dmix, dsum, turned, qh, kh, vh, dh, kt, dq_s, dk_s, dv_s, dqt):
+    slots, d = x_ref.shape
+    tile = 256
+    tiles = slots // tile
+    pairs = HEADS // 2
+    blocks = 16
+    head_row = lax.broadcasted_iota(jnp.int32, (128, d), 0)
+    head_col = lax.broadcasted_iota(jnp.int32, (128, d), 1)
+    pick = jnp.where(head_col // HEAD_DIM == head_row, 1.0, 0.0).astype(BF16)
+
+    def first(t, carry):
+        rows = row_block(t, tile)
+        low = dhid_ref[rows, :].astype(BF16)
+        dhl[rows, :] = low
+        grad = nt(low, wo_ref[...]).astype(BF16)
+        dmix[rows, :] = grad
+        mixed = mixed_ref[rows, :]
+        prod = grad.astype(F32) * mixed.astype(F32)
+        high = prod.astype(BF16)
+        rest = (prod - high.astype(F32)).astype(BF16)
+        dsum[:, rows] = nt(pick, high) + nt(pick, rest)
+        permuted_store(turned, rows, mixed, d // blocks)
+        return carry
+
+    lax.fori_loop(0, tiles, first, 0)
+
+    def weight_grads(target, right):
+        def step(n, carry):
+            cols = row_block(n, 256)
+            target[:, cols] = nn(turned[...], right[:, cols]).astype(BF16)
+            return carry
+
+        lax.fori_loop(0, d // 256, step, 0)
+
+    weight_grads(gout_ref, dhl)
+    count = count_ref[0]
+    lane = lanes_of(slots)
+    slot = lax.broadcasted_iota(jnp.int32, (slots, 128), 0)
+    bias = jnp.where(slot < count, 0.0, -1e30)
+
+    def pair_step(p, carry):
+        cols = row_block(p, 128)
+        kp = k_ref[:, cols].astype(F32)
+        kh[0], kh[1] = head_masks(kp, lane, bias)
+        for h in range(2):
+            own = (lane < 64) if h == 0 else (lane >= 64)
+            kt[h] = jnp.transpose(jnp.where(own, kp, 0.0)).astype(BF16)
+        qp = q_ref[:, cols].astype(F32)
+        qh[0] = jnp.where(lane == 64, 1.0, qp).astype(BF16)
+        qh[1] = jnp.where(lane == 0, 1.0, qp).astype(BF16)
+        qh[2], qh[3] = head_masks(qp, lane, 0.0)
+        vh[0], vh[1] = head_masks(v_ref[:, cols].astype(F32), lane, 0.0)
+        grad_pair = dmix[:, cols]
+        dh[0], dh[1] = head_masks(grad_pair.astype(F32), lane, 0.0)
+        dqt[...] = jnp.zeros_like(dqt)
+
+        def tile_step(t, carry):
+            rows = row_block(t, tile)
+            d_k = d_v = None
+            for h in range(2):
+                score = nt(kh[h, rows, :], qh[h])
+                weight = jnp.exp(score - lse_ref[pl.ds(2 * p + h, 1), :])
+                d_att = nt(vh[h, rows, :], dmix[:, cols])
+                d_score = (weight * (d_att - dsum[pl.ds(2 * p + h, 1), :])).astype(BF16)
+                part_v = nn(weight.astype(BF16), dh[h])
+                part_k = nn(d_score, qh[2 + h])
+                d_v = part_v if d_v is None else d_v + part_v
+                d_k = part_k if d_k is None else d_k + part_k
+                dqt[...] += nn(kt[h, :, rows], d_score)
+            dk_s[rows, cols] = d_k.astype(BF16)
+            dv_s[rows, cols] = d_v.astype(BF16)
+            return carry
+
+        lax.fori_loop(0, tiles, tile_step, 0)
+        dq_s[:, cols] = jnp.transpose(dqt[...]).astype(BF16)
+        return carry
+
+    lax.fori_loop(0, pairs, pair_step, 0)
+    ggain_ref[...] = jnp.zeros_like(ggain_ref)
+
+    def last(t, carry):
+        rows = row_block(t, tile)
+        permuted_store(turned, rows, normed_ref[rows, :], d // blocks)
+        x = x_ref[rows, :].astype(F32)
+        r = lax.rsqrt(jnp.mean(x * x, axis=-1, keepdims=True) + epsilon)
+        dn = nt(dq_s[rows, :], wq_ref[...]) + nt(dk_s[rows, :], wk_ref[...]) + nt(dv_s[rows, :], wv_ref[...])
+        scaled = dn * gain_ref[...]
+        mean = jnp.mean(scaled * x, axis=-1, keepdims=True)
+        gplots_ref[rows, :] = (dhid_ref[rows, :] + r * scaled - x * (r * r * r * mean)).astype(BF16)
+        ggain_ref[...] += jnp.sum(dn * x * r, axis=0, keepdims=True)
+        return carry
+
+    lax.fori_loop(0, tiles, last, 0)
+    weight_grads(gq_ref, dq_s)
+    weight_grads(gk_ref, dk_s)
+    weight_grads(gv_ref, dv_s)
+
+
+def call(kernel, outs, scratch, args, scalars=1):
+    return pl.pallas_call(
+        kernel,
+        out_shape=[jax.ShapeDtypeStruct(shape, dtype) for shape, dtype in outs],
+        in_specs=[pl.BlockSpec(memory_space=pltpu.SMEM)] * scalars
+        + [pl.BlockSpec(memory_space=pltpu.VMEM)] * (len(args) - scalars),
+        out_specs=[pl.BlockSpec(memory_space=pltpu.VMEM)] * len(outs),
+        scratch_shapes=scratch,
+        compiler_params=pltpu.CompilerParams(vmem_limit_bytes=VMEM_BYTES),
+    )(*args)
+
+
+def unpermute(grad, rows):
+    cols = grad.shape[1]
+    return grad.reshape(2, 2, -1, rows, cols).transpose(2, 1, 0, 3, 4).reshape(-1, cols)
+
+
+def body_plot(plots, plot_grid, query_weight, key_weight, value_weight, out_weight, gate_weight, up_weight, down_weight,
+              gain_attn, gain_mlp, cotangent):
+    rows, d = query_weight.shape
+    ff = gate_weight.shape[1]
+    rows_down = down_weight.shape[0]
+    x = lax.all_to_all(plots, "narrow", 0, 1, tiled=True)[0]
+    cot = lax.all_to_all(cotangent, "narrow", 0, 1, tiled=True)[0]
+    slots = x.shape[0]
+    counts = plot_grid[:, 0] * plot_grid[:, 1]
+    count = lax.dynamic_slice(counts, (lax.axis_index("narrow"),), (1,))
+    gather = functools.partial(lax.all_gather, axis_name="wide", axis=0, tiled=True)
+    gains = lax.all_gather(jnp.stack([gain_attn, gain_mlp]), "wide", axis=1, tiled=True).astype(F32)
+    wq, wk, wv, wo = gather(query_weight), gather(key_weight), gather(value_weight), gather(out_weight)
+    wg, wu, wd = gather(gate_weight), gather(up_weight), gather(down_weight)
+    act = lambda dtype=BF16: ((slots, d), dtype)
+    vm = lambda shape, dtype=BF16: pltpu.VMEM(shape, dtype)
+    q, k, v, normed, mixed, lse, hidden = call(
+        attend_forward,
+        [act(), act(), act(), act(), act(), ((128, slots), F32), act(F32)],
+        [vm((2, slots, 128)), vm((2, slots, 128)), vm((2, slots, 256)), vm((slots, 128), F32)],
+        (count, x, gains[0:1], wq, wk, wv, wo),
+    )
+    output, dhid, g_down, g_gate, g_up, gg_mlp = call(
+        mlp_both,
+        [act(), act(F32), ((ff, d), BF16), ((d, ff), BF16), ((d, ff), BF16), ((1, d), F32)],
+        [vm((d, slots)), vm((ff, slots)), vm((slots, ff)), vm((slots, ff))],
+        (hidden, cot, gains[1:2], wg, wu, wd), 0,
+    )
+    gplots, g_q, g_k, g_v, g_out, gg_attn = call(
+        attend_backward,
+        [act(), ((d, d), BF16), ((d, d), BF16), ((d, d), BF16), ((d, d), BF16), ((1, d), F32)],
+        [vm((slots, d)), vm((slots, d)), vm((128, slots), F32), vm((d, slots)), vm((4, slots, 128)), vm((2, slots, 128)),
+         vm((2, slots, 128)), vm((2, slots, 128)), vm((2, 128, slots)), vm((slots, d)), vm((slots, d)), vm((slots, d)),
+         vm((128, slots), F32)],
+        (count, x, gains[0:1], wq, wk, wv, wo, q, k, v, normed, mixed, lse, dhid),
+    )
+
+    def reduce(grad, rows):
+        part = lax.psum_scatter(unpermute(grad, rows), "wide", scatter_dimension=0, tiled=True)
+        return lax.psum(part, "narrow").astype(F32)
+
+    def reduce_gain(grad):
+        total = lax.psum(grad[0], ("wide", "narrow"))
+        return lax.dynamic_slice(total, (lax.axis_index("wide") * rows,), (rows,))
+
+    back = lambda value: lax.all_to_all(value[None], "narrow", 1, 0, tiled=True)
+    return (back(output), back(gplots), reduce(g_q, rows), reduce(g_k, rows), reduce(g_v, rows), reduce(g_out, rows),
+            reduce(g_gate, rows), reduce(g_up, rows), reduce(g_down, rows_down), reduce_gain(gg_attn), reduce_gain(gg_mlp))
+
+
+def body_for(mesh):
+    plots_fit = mesh.shape["narrow"] == 2 and mesh.shape["wide"] == 16
+
+    def body(plots, *rest):
+        if plots_fit and plots.shape == (2, 512, HEADS * HEAD_DIM):
+            return body_plot(plots, *rest)
+        return body_general(plots, *rest)
+
+    return body
+
+
 def solution(mesh):
     return jax.shard_map(
-        body,
+        body_for(mesh),
         mesh=mesh,
         in_specs=(
             P("wide", "narrow", None),

time: 1190 us -> 1010 us (0.85)
  matrix products: 418 us -> 0 us
  Pallas kernels: 0 us -> 176 us
  waiting for transfers between devices: 592 us -> 625 us
  starting transfers between devices: 1.55 us -> 17.9 us
  blocking collectives: 69.7 us -> 82.1 us
    dot_general x119 -> x0, matrix products: 368 us -> none  [the longest x24 78.1 us: head_forward(): jnp.einsum('pqk,pke->pqe', (exponent / total).astype(jnp.bfloat16), value...]
    pallas_call x0 -> x3, Pallas kernels: none -> 176 us  [call(): pl.pallas_call(kernel, out_shape=[jax.ShapeDtypeStruct(shape, dtype) for...]
    unnamed x2 -> x0, blocking collectives: 64.8 us -> none
    psum x1, blocking collectives: 4.92 us -> 60.3 us  [reduce_gain(): total = lax.psum(grad[0], ('wide', 'narrow'))]
    sub x12 -> x0, matrix products: 50.5 us -> none  [head_forward(): exponent = jnp.exp(scores - row_max)]
    reduce_scatter x9 -> x7, waiting for transfers between devices: 360 us -> 399 us  [reduce(): lax.psum_scatter(unpermute(grad, rows), 'wide', scatter_dimension=0, tile...]
    unnamed x0 -> x3, other arithmetic: none -> 32.6 us
    all_gather x9 -> x7, waiting for transfers between devices: 227 us -> 202 us  [the longest x3 96.1 us: body_plot(): wg, wu, wd = (gather(gate_weight), gather(up_weight), gather(down_weight))]
  transfers between devices with their start and end apart: 19 -> 19, of which waited for: 14 -> 14; matrix products, arithmetic and copies ran while one was open for 27% -> 7% of each run, Pallas kernels for 0% -> 4%
where the time goes in v1:
time: 1010 us; the launch traced here: 998 us
  waiting for transfers between devices  625 us (62%)
  Pallas kernels  176 us (17%)
  blocking collectives  82.1 us (8%)
  local copies, waits for them, and re-layouts  41.7 us (4%)
  other arithmetic  40.5 us (4%)
  starting transfers between devices  17.9 us (2%)
  between operations  14.4 us (1%)
    reduce_scatter x7, waiting for transfers between devices, reduce(): lax.psum_scatter(unpermute(grad, rows), 'wide', scatter_dimension=0, tile...  399 us
    pallas_call x3, Pallas kernels, call(): pl.pallas_call(kernel, out_shape=[jax.ShapeDtypeStruct(shape, dtype) for...  176 us
    all_gather x3, waiting for transfers between devices, body_plot(): wg, wu, wd = (gather(gate_weight), gather(up_weight), gather(down_weight))  96.1 us
    psum x1, blocking collectives, reduce_gain(): total = lax.psum(grad[0], ('wide', 'narrow'))  60.3 us
    all_gather x1, waiting for transfers between devices, body_plot(): gather(out_weight)  39.6 us
    all_gather x1, waiting for transfers between devices, body_plot(): gather(query_weight)  39.5 us
    unnamed x3, other arithmetic  32.6 us
    all_gather x1, waiting for transfers between devices, body_plot(): gather(value_weight)  26.7 us
  transfers between devices with their start and end apart: 19, of which 14 were waited for; matrix products, arithmetic and copies ran while one was open for 7% of the time, Pallas kernels for 4%

profile of v1, /device:TPU:0, one launch (start us, length us, event | category | flops | bytes accessed | tf_op | source)
XLA Modules:
  0.0 998.2 jit_solution(18398756093126629318)
XLA Ops:
  11.9 4.2 all-to-all-start
  16.1 20.1 %all-to-all-done = bf16[2,512,768]{2,1,0:T(8,128)(2,1)S(1)} async-done(((bf16[2,512,768]{2,1,0:T(8,128)(2,1)}), bf16[2,512,768]{2,1,0:T(8,128)(2,1)S(1)}, u32[]{:S(2)}, u32[]{:S(2)}) %all-to-all-start) | async-done | bytes 1572896 | tf_op jit(solution)/shard_map/all_to_all | solution.py:596
  37.4 3.7 all-to-all-start.1
  41.2 21.7 %all-gather = bf16[16,48,2]{1,2,0:T(2,128)(2,1)S(1)} all-gather(bf16[1,48,2]{1,2,0:T(2,128)(2,1)S(1)} %maximum_bitcast_fusion), channel_id=1, replica_groups=mesh['wide'=16,'narrow'=2] {'wide'}, dimensions={0}, use_global_device_ids=true | all-gather | bytes 3264 | tf_op jit(solution)/shard_map/all_gather | solution.py:602
  64.2 26.7 %all-gather.13.cloned.1.call-done.wv_ref = bf16[768,768]{1,0:T(8,128)(2,1)} async-done(((bf16[48,768]{1,0:T(8,128)(2,1)}), bf16[768,768]{1,0:T(8,128)(2,1)}) %all-gather.13.cloned.1.call-update) | async-done | bytes 1179664 | tf_op jit(solution)/shard_map/all_gather | solution.py:603
  90.9 39.6 %all-gather.15.cloned.1.call-done.wo_ref = bf16[768,768]{1,0:T(8,128)(2,1)} async-done(((bf16[48,768]{1,0:T(8,128)(2,1)}), bf16[768,768]{1,0:T(8,128)(2,1)}) %all-gather.15.cloned.1.call-update) | async-done | bytes 1179664 | tf_op jit(solution)/shard_map/all_gather | solution.py:603
  130.5 39.5 %all-gather.9.cloned.1.call-done.wq_ref = bf16[768,768]{1,0:T(8,128)(2,1)} async-done(((bf16[48,768]{1,0:T(8,128)(2,1)}), bf16[768,768]{1,0:T(8,128)(2,1)}) %all-gather.9.cloned.1.call-update) | async-done | bytes 1179664 | tf_op jit(solution)/shard_map/all_gather | solution.py:603
  170.0 42.9 %shard_map.203 = (bf16[1024,768]{1,0:T(8,128)(2,1)}, bf16[1024,768]{1,0:T(8,128)(2,1)}, bf16[1024,768]{1,0:T(8,128)(2,1)}, bf16[1024,768]{1,0:T(8,128)(2,1)}, bf...) custom-call(s32[1]{0:T(128)} %bitcast.count_ref, bf16[1024,768]{1,0:T(8,128)(2,1)} %bitcast.52, ...), custom_call_target="tpu_custom_call" | custom-call | tf_op jit(solution)/shard_map/pallas_call | solution.py:575
  212.9 3.4 all-gather.17.cloned.1.call-done.wg_ref
  216.3 46.4 %all-gather.19.cloned.1.call-done.wu_ref = bf16[768,2048]{1,0:T(8,128)(2,1)} async-done(((bf16[48,2048]{1,0:T(8,128)(2,1)}), bf16[768,2048]{1,0:T(8,128)(2,1)}) %all-gather.19.cloned.1.call-update) | async-done | bytes 3145744 | tf_op jit(solution)/shard_map/all_gather | solution.py:604
  262.7 46.3 %all-gather.21.cloned.1.call-done.wd_ref = bf16[2048,768]{1,0:T(8,128)(2,1)} async-done(((bf16[128,768]{1,0:T(8,128)(2,1)}), bf16[2048,768]{1,0:T(8,128)(2,1)}) %all-gather.21.cloned.1.call-update) | async-done | bytes 3145744 | tf_op jit(solution)/shard_map/all_gather | solution.py:604
  309.0 65.0 %shard_map.204 = (bf16[1024,768]{1,0:T(8,128)(2,1)}, f32[1024,768]{1,0:T(8,128)}, bf16[2048,768]{1,0:T(8,128)(2,1)}, bf16[768,2048]{1,0:T(8,128)(2,1)}, bf16[768,2048]{1,0:T(8,128)(2,1)}, /*index=5*/f32[1,768]{1,0:T(1,128)}) custom-call(f32[1024,768]{1,0:T(8,128)} %get-tuple-element.30.hidden_ref, bf16[1024,768]{1,0:T(8,128)(2,1)} %bitcast.61, ...), custom_call_target="tpu_custom_call" | custom-call | tf_op jit(solution)/shard_map/pallas_call | solution.py:575
  374.0 68.5 %shard_map.205 = (bf16[1024,768]{1,0:T(8,128)(2,1)}, bf16[768,768]{1,0:T(8,128)(2,1)}, bf16[768,768]{1,0:T(8,128)(2,1)}, bf16[768,768]{1,0:T(8,128)(2,1)}, bf16[768,768]{1,0:T(8,128)(2,1)}, /*index=5*/f32[1,768]{1,0:T(1,128)}) custom-call(s32[1]{0:T(128)} %bitcast.count_ref, bf16[1024,768]{1,0:T(8,128)(2,1)} %bitcast.53, ...), custom_call_target="tpu_custom_call" | custom-call | tf_op jit(solution)/shard_map/pallas_call | solution.py:575
  442.5 2.5 copy.55
  448.0 2.5 copy.54
  460.2 3.9 copy.66
  464.6 21.0 %reduce.3 = bf16[1024,768]{1,0:T(8,128)(2,1)} reduce(bf16[1024,1,768]{2,1,0:T(2,128)(2,1)S(1)} %bitcast.57, bf16[]{:T(256)} %broadcast.2), dimensions={1}, to_apply=%bitcast.50.reduce_sub_computation | reduce | bytes 3145730
  485.5 2.5 reshape.101
  488.0 4.6 all-to-all-start.3
  492.7 9.3 reduce-scatter.10.cloned.1.call-done
  502.1 60.7 %reduce-scatter.12.cloned.1.call-done = bf16[48,768]{1,0:T(8,128)(2,1)} async-done(((bf16[768,768]{1,0:T(8,128)(2,1)}), bf16[48,768]{1,0:T(8,128)(2,1)}) %reduce-scatter.12.cloned.1.call-update) | async-done | bytes 73744 | tf_op jit(solution)/shard_map/reduce_scatter | solution.py:629
  562.8 60.6 %reduce-scatter.14.cloned.1.call-done = bf16[48,768]{1,0:T(8,128)(2,1)} async-done(((bf16[768,768]{1,0:T(8,128)(2,1)}), bf16[48,768]{1,0:T(8,128)(2,1)}) %reduce-scatter.14.cloned.1.call-update) | async-done | bytes 73744 | tf_op jit(solution)/shard_map/reduce_scatter | solution.py:629
  623.4 61.3 %reduce-scatter.8.cloned.1.call-done = bf16[48,768]{1,0:T(8,128)(2,1)} async-done(((bf16[768,768]{1,0:T(8,128)(2,1)}), bf16[48,768]{1,0:T(8,128)(2,1)}) %reduce-scatter.8.cloned.1.call-update) | async-done | bytes 73744 | tf_op jit(solution)/shard_map/reduce_scatter | solution.py:629
  684.7 68.9 %reduce-scatter.16.cloned.1.call-done = bf16[48,2048]{1,0:T(8,128)(2,1)} async-done(((bf16[768,2048]{1,0:T(8,128)(2,1)}), bf16[48,2048]{1,0:T(8,128)(2,1)}) %reduce-scatter.16.cloned.1.call-update) | async-done | bytes 196624 | tf_op jit(solution)/shard_map/reduce_scatter | solution.py:629
  753.6 69.0 %reduce-scatter.18.cloned.1.call-done = bf16[48,2048]{1,0:T(8,128)(2,1)} async-done(((bf16[768,2048]{1,0:T(8,128)(2,1)}), bf16[48,2048]{1,0:T(8,128)(2,1)}) %reduce-scatter.18.cloned.1.call-update) | async-done | bytes 196624 | tf_op jit(solution)/shard_map/reduce_scatter | solution.py:629
  822.6 68.9 %reduce-scatter.20.cloned.1.call-done = bf16[128,768]{1,0:T(8,128)(2,1)} async-done(((bf16[2048,768]{1,0:T(8,128)(2,1)}), bf16[128,768]{1,0:T(8,128)(2,1)}) %reduce-scatter.20.cloned.1.call-update) | async-done | bytes 196624 | tf_op jit(solution)/shard_map/reduce_scatter | solution.py:629
  891.5 3.8 copy.67
  895.4 11.6 %reduce.2 = bf16[1024,768]{1,0:T(8,128)(2,1)} reduce(bf16[1024,1,768]{2,1,0:T(2,128)(2,1)S(1)} %bitcast.58, bf16[]{:T(256)} %broadcast.2), dimensions={1}, to_apply=%bitcast.51.reduce_sub_computation | reduce | bytes 3145730
  909.5 4.8 all-to-all-start.2
  914.3 60.3 %all-reduce = (f32[768]{0:T(1024)S(1)}, f32[768]{0:T(1024)S(1)}) all-reduce(f32[768]{0:T(1024)S(1)} %reduce, f32[768]{0:T(1024)S(1)} %reduce.1), channel_id=1, replica_groups=mesh['wide'=16,'narrow'=2] {'wide','narrow'}, use_global_device_ids=true, to_apply=%region_14.0 | all-reduce | flops 1536 | bytes 12288 | tf_op jit(solution)/shard_map/psum | solution.py:633
  975.8 2.5 reshape.102
  979.7 2.5 reshape.100
  (93 shorter events, 34.5 us)
Async XLA Ops:
  7.2 57.0 %all-gather.11.cloned.1.call-start = ((), (), s32[]{:S(2)}) async-start(), calls=%async_computation.12 | async-start | bytes 1253376 | tf_op jit(solution)/shard_map/all_gather | solution.py:603
  7.9 83.0 %all-gather.13.cloned.1.call-start = ((), (), s32[]{:S(2)}) async-start(), calls=%async_computation.13 | async-start | bytes 1253376 | tf_op jit(solution)/shard_map/all_gather | solution.py:603
  8.7 121.9 %all-gather.15.cloned.1.call-start = ((), (), s32[]{:S(2)}) async-start(), calls=%async_computation.14 | async-start | bytes 1253376 | tf_op jit(solution)/shard_map/all_gather | solution.py:603
  9.4 160.6 %all-gather.9.cloned.1.call-start = ((), (), s32[]{:S(2)}) async-start(), calls=%async_computation.11 | async-start | bytes 1253376 | tf_op jit(solution)/shard_map/all_gather | solution.py:603
  10.0 206.3 %all-gather.17.cloned.1.call-start = ((), (), s32[]{:S(2)}) async-start(), calls=%async_computation.15 | async-start | bytes 3342336 | tf_op jit(solution)/shard_map/all_gather | solution.py:604
  10.6 252.1 %all-gather.19.cloned.1.call-start = ((), (), s32[]{:S(2)}) async-start(), calls=%async_computation.16 | async-start | bytes 3342336 | tf_op jit(solution)/shard_map/all_gather | solution.py:604
  11.1 297.9 %all-gather.21.cloned.1.call-start = ((), (), s32[]{:S(2)}) async-start(), calls=%async_computation.17 | async-start | bytes 3342336 | tf_op jit(solution)/shard_map/all_gather | solution.py:604
  11.9 24.4 %all-to-all-start = ((bf16[2,512,768]{2,1,0:T(8,128)(2,1)}), bf16[2,512,768]{2,1,0:T(8,128)(2,1)S(1)}, u32[]{:S(2)}, u32[]{:S(2)}) async-start(bf16[2,512,768]{2,1,0:T(8,128)(2,1)} %param.12), calls=%async_computation | async-start | bytes 3145728 | tf_op jit(solution)/shard_map/all_to_all | solution.py:596
  16.1 25.0 %copy-start.14 = (bf16[48]{0:T(256)(128)(2,1)S(1)}, bf16[48]{0:T(256)(128)(2,1)}, u32[]{:S(2)}) copy-start(bf16[48]{0:T(256)(128)(2,1)} %param.22) | copy-start | bytes 292
  16.1 25.0 %copy-start.15 = (bf16[48]{0:T(256)(128)(2,1)S(1)}, bf16[48]{0:T(256)(128)(2,1)}, u32[]{:S(2)}) copy-start(bf16[48]{0:T(256)(128)(2,1)} %param.21) | copy-start | bytes 292
  16.1 46.9 %copy-start.11 = (s32[2,2]{1,0:T(2,128)S(1)}, s32[2,2]{1,0:T(2,128)}, u32[]{:S(2)}) copy-start(s32[2,2]{1,0:T(2,128)} %param.13) | copy-start | bytes 52
  37.4 175.5 %all-to-all-start.1 = ((bf16[2,512,768]{2,1,0:T(8,128)(2,1)}), bf16[2,512,768]{2,1,0:T(8,128)(2,1)S(1)}, u32[]{:S(2)}, u32[]{:S(2)}) async-start(bf16[2,512,768]{2,1,0:T(8,128)(2,1)} %param.23), calls=%async_computation.1 | async-start | bytes 3145728 | tf_op jit(solution)/shard_map/all_to_all | solution.py:597
  41.1 461.0 %reduce-scatter.10.cloned.1.call-start = ((), (), s32[]{:S(2)}) async-start(), calls=%async_computation.19 | async-start | bytes 1253376 | tf_op jit(solution)/shard_map/reduce_scatter | solution.py:629
  212.9 96.1 %copy-start.1 = (bf16[2,512,768]{2,1,0:T(8,128)(2,1)}, bf16[2,512,768]{2,1,0:T(8,128)(2,1)S(1)}, u32[]{:S(2)}) copy-start(bf16[2,512,768]{2,1,0:T(8,128)(2,1)S(1)} %all-to-all-done.1) | copy-start | bytes 4718596
  442.5 2.6 copy-start.6
  445.0 117.8 %reduce-scatter.12.cloned.1.call-start = ((), (), s32[]{:S(2)}) async-start(), calls=%async_computation.20 | async-start | bytes 1253376 | tf_op jit(solution)/shard_map/reduce_scatter | solution.py:629
  446.2 177.2 %reduce-scatter.14.cloned.1.call-start = ((), (), s32[]{:S(2)}) async-start(), calls=%async_computation.21 | async-start | bytes 1253376 | tf_op jit(solution)/shard_map/reduce_scatter | solution.py:629
  447.9 236.8 %reduce-scatter.8.cloned.1.call-start = ((), (), s32[]{:S(2)}) async-start(), calls=%async_computation.18 | async-start | bytes 1253376 | tf_op jit(solution)/shard_map/reduce_scatter | solution.py:629
  447.9 2.6 copy-start.4
  450.5 303.1 %reduce-scatter.16.cloned.1.call-start = ((), (), s32[]{:S(2)}) async-start(), calls=%async_computation.22 | async-start | bytes 3342336 | tf_op jit(solution)/shard_map/reduce_scatter | solution.py:629
  452.5 370.1 %reduce-scatter.18.cloned.1.call-start = ((), (), s32[]{:S(2)}) async-start(), calls=%async_computation.23 | async-start | bytes 3342336 | tf_op jit(solution)/shard_map/reduce_scatter | solution.py:629
  456.4 1.9 copy-start.2
  456.4 435.1 %reduce-scatter.20.cloned.1.call-start = ((), (), s32[]{:S(2)}) async-start(), calls=%async_computation.24 | async-start | bytes 3342336 | tf_op jit(solution)/shard_map/reduce_scatter | solution.py:629
  488.0 421.4 %all-to-all-start.3 = ((bf16[2,2,196608]{2,1,0:T(2,128)(2,1)}), bf16[2,2,196608]{2,1,0:T(2,128)(2,1)}, u32[]{:S(2)}, u32[]{:S(2)}) async-start(bf16[2,2,196608]{2,1,0:T(2,128)(2,1)} %reshape.101), calls=%async_computation.3 | async-start | bytes 3145728 | tf_op jit(solution)/shard_map/all_to_all | solution.py:636
  492.7 490.9 %all-reduce.4.cloned.1.call-start = ((), (), s32[]{:S(2)}) async-start(), calls=%async_computation.25 | async-start | bytes 1769472 | tf_op jit(solution)/shard_map/psum | solution.py:630
  909.5 4.8 copy-start.13
  909.5 4.8 copy-start.12
  909.5 70.2 %all-to-all-start.2 = ((bf16[2,2,196608]{2,1,0:T(2,128)(2,1)}), bf16[2,2,196608]{2,1,0:T(2,128)(2,1)}, u32[]{:S(2)}, u32[]{:S(2)}) async-start(bf16[2,2,196608]{2,1,0:T(2,128)(2,1)} %reshape.99), calls=%async_computation.2 | async-start | bytes 3145728 | tf_op jit(solution)/shard_map/all_to_all | solution.py:636
  983.6 5.2 copy-start.10
  983.6 5.8 copy-start.9
  983.6 6.5 copy-start.8
  983.6 7.2 copy-start.7
  (3 other events, 4.8 us)
Sparse Core Ops, SparseCore 0:
  10.3 41.0 all-gather.10
  53.6 37.2 all-gather.12
  93.2 37.2 all-gather.14
  132.7 37.2 all-gather.8
  172.1 44.1 all-gather.16
  218.4 44.2 all-gather.18
  265.0 43.9 all-gather.20
  445.1 56.9 reduce-scatter.9
  505.7 57.0 reduce-scatter.11
  566.2 57.0 reduce-scatter.13
  627.6 57.1 reduce-scatter.7
  688.4 65.1 reduce-scatter.15
  757.4 65.1 reduce-scatter.17
  826.3 65.2 reduce-scatter.19
  894.1 46.4 all-reduce.3

commit v2 on v1

--- a/solution.py
+++ b/solution.py
@@ -336,26 +336,176 @@
     return first.astype(BF16), second.astype(BF16)
 
 
-def attend_forward(count_ref, x_ref, gain_ref, wq_ref, wk_ref, wv_ref, wo_ref,
-                   q_ref, k_ref, v_ref, normed_ref, mixed_ref, lse_ref, hidden_ref,
-                   qh, kh, vh, lse_cols):
-    slots = x_ref.shape[0]
+MESH_ID = pl.DeviceIdType.MESH
+
+
+class Place:
+    def __init__(self):
+        wide, self.y = lax.axis_index("wide"), lax.axis_index("narrow")
+        self.z, self.x, self.c = wide // 4, (wide // 2) % 2, wide % 2
+        self.wide = wide
+
+    def block(self, z, x, c):
+        return (z * 2 + x) * 2 + c
+
+    def other_z(self, j):
+        z = self.z
+        return (z + 1 - 2 * (z % 2), (z + 2) % 4, 3 - z)[j]
+
+    def to_z(self, j):
+        return (self.block(self.other_z(j), self.x, self.c), self.y)
+
+    def to_x(self):
+        return (self.block(self.z, 1 - self.x, self.c), self.y)
+
+    def to_core(self):
+        return (self.block(self.z, self.x, 1 - self.c), self.y)
+
+    def to_y(self):
+        return (self.wide, 1 - self.y)
+
+    def greet(self):
+        barrier = pltpu.get_barrier_semaphore()
+        partners = [self.to_z(0), self.to_z(1), self.to_z(2), self.to_x(), self.to_core(), self.to_y()]
+        for partner in partners:
+            pl.semaphore_signal(barrier, inc=1, device_id=partner, device_id_type=MESH_ID)
+        pl.semaphore_wait(barrier, len(partners))
+
+
+class Gather:
+    def __init__(self, place, full, send, recv):
+        self.place, self.full, self.sends, self.recvs = place, full, send, recv
+        self.slot = 0
+
+    def copy(self, block, target, slot):
+        return pltpu.make_async_remote_copy(
+            src_ref=self.full.at[block], dst_ref=self.full.at[block], send_sem=self.sends.at[slot],
+            recv_sem=self.recvs.at[block], device_id=target, device_id_type=MESH_ID)
+
+    def send(self, block, target):
+        self.copy(block, target, self.slot).start()
+        self.slot += 1
+
+    def wait(self, block):
+        self.copy(block, self.place.to_core(), 0).wait_recv()
+
+    def start(self):
+        p = self.place
+        own = p.block(p.z, p.x, p.c)
+        for j in (2, 1, 0):
+            self.send(own, p.to_z(j))
+        self.send(own, p.to_x())
+        self.send(own, p.to_core())
+
+    def pass_z(self, j):
+        p = self.place
+        block = p.block(p.other_z(j), p.x, p.c)
+        self.wait(block)
+        self.send(block, p.to_x())
+        self.send(block, p.to_core())
+
+    def pass_x(self, j):
+        p = self.place
+        block = p.block(p.z if j == 3 else p.other_z(j), 1 - p.x, p.c)
+        self.wait(block)
+        self.send(block, p.to_core())
+
+    def end(self):
+        p = self.place
+        for z in range(4):
+            for x in range(2):
+                self.wait(p.block(z, x, 1 - p.c))
+
+    def sent(self):
+        for slot in range(15):
+            self.copy(0, self.place.to_core(), slot).wait_send()
+
+
+def gather_forward(count_ref, plots_ref, cot_ref, gain_a_ref, gain_m_ref, own_q, own_k, own_v, own_o, own_g, own_u, own_d,
+                   q_ref, k_ref, v_ref, normed_ref, mixed_ref, lse_ref, hidden_ref, x_ref, cot_out, gains_ref,
+                   out_q, out_k, out_v, out_o, out_g, out_u, out_d,
+                   qh, kh, vh, lse_cols, wq, wk, wv, wo, wg, wu, wd, wgain, sends, recvs, half_sems, out_sems):
+    half = plots_ref.shape[1]
+    slots = 2 * half
     tile = 256
     tiles = slots // tile
     pairs = HEADS // 2
-
-    def project(t, carry):
+    d = plots_ref.shape[2]
+    place = Place()
+    fulls = (wgain, wq, wk, wv, wo, wg, wu, wd)
+    for full, own in zip(fulls[1:], (own_q, own_k, own_v, own_o, own_g, own_u, own_d)):
+        full[place.wide] = own[...]
+    wgain[place.wide, 0:1, 0:own_q.shape[0]] = gain_a_ref[...].astype(F32)
+    wgain[place.wide, 1:2, 0:own_q.shape[0]] = gain_m_ref[...].astype(F32)
+    gathers = [Gather(place, full, sends.at[i], recvs.at[i]) for i, full in enumerate(fulls)]
+    g_gain, g_q, g_k, g_v, g_o, g_g, g_u, g_d = gathers
+    mine = pl.ds(pl.multiple_of(place.y * half, half), half)
+
+    def half_copy(source, target, i):
+        return pltpu.make_async_remote_copy(
+            src_ref=source.at[1 - place.y], dst_ref=target.at[mine], send_sem=half_sems.at[2 * i],
+            recv_sem=half_sems.at[2 * i + 1], device_id=place.to_y(), device_id_type=MESH_ID)
+
+    place.greet()
+    x_copy, cot_copy = half_copy(plots_ref, x_ref, 0), half_copy(cot_ref, cot_out, 1)
+    x_copy.start()
+    for g in (g_gain, g_q, g_k, g_v):
+        g.start()
+    x_ref[mine, :] = plots_ref[place.y]
+    cot_out[mine, :] = cot_ref[place.y]
+
+    def relay_z(g):
+        for j in range(3):
+            g.pass_z(j)
+
+    def relay_x(g):
+        for j in (3, 0, 1, 2):
+            g.pass_x(j)
+
+    relay_z(g_gain)
+    relay_z(g_q)
+    g_o.start()
+    relay_z(g_k)
+    g_g.start()
+    relay_x(g_gain)
+    relay_x(g_q)
+    relay_z(g_v)
+    g_gain.end()
+    rows_own = own_q.shape[0]
+    for w in range(16):
+        for i in range(2):
+            gains_ref[i:i + 1, w * rows_own:(w + 1) * rows_own] = wgain[w, i:i + 1, 0:rows_own]
+    x_copy.wait()
+    cot_copy.start()
+
+    def normalise(t, carry):
         rows = row_block(t, tile)
         x = x_ref[rows, :].astype(F32)
         r = lax.rsqrt(jnp.mean(x * x, axis=-1, keepdims=True) + epsilon)
-        normed = (x * r * gain_ref[...]).astype(BF16)
-        normed_ref[rows, :] = normed
-        q_ref[rows, :] = nn(normed, wq_ref[...]).astype(BF16)
-        k_ref[rows, :] = nn(normed, wk_ref[...]).astype(BF16)
-        v_ref[rows, :] = nn(normed, wv_ref[...]).astype(BF16)
+        normed_ref[rows, :] = (x * r * gains_ref[0:1, :]).astype(BF16)
         return carry
 
-    lax.fori_loop(0, tiles, project, 0)
+    lax.fori_loop(0, tiles, normalise, 0)
+
+    def project(target, full):
+        def step(t, carry):
+            rows = row_block(t, tile)
+            target[rows, :] = nn(normed_ref[rows, :], full[...].reshape(d, d)).astype(BF16)
+            return carry
+
+        lax.fori_loop(0, tiles, step, 0)
+
+    relay_x(g_k)
+    g_q.end()
+    project(q_ref, wq)
+    relay_x(g_v)
+    g_k.end()
+    project(k_ref, wk)
+    relay_z(g_o)
+    g_u.start()
+    g_v.end()
+    project(v_ref, wv)
+
     count = count_ref[0]
     lane = lanes_of(slots)
     slot = lax.broadcasted_iota(jnp.int32, (slots, 128), 0)
@@ -363,43 +513,69 @@
     lse_cols[...] = jnp.zeros_like(lse_cols)
     for h in range(2):
         vh[h, :, 128:] = jnp.ones((slots, 128), BF16)
-
-    def pair_step(p, carry):
+    hooks = {
+        0: [lambda: g_g.pass_z(0)], 1: [lambda: relay_x(g_o)], 2: [lambda: g_g.pass_z(1)], 4: [lambda: g_g.pass_z(2), lambda: g_d.start()],
+        5: [lambda: g_g.pass_x(3)], 6: [lambda: g_g.pass_x(0)], 7: [lambda: g_g.pass_x(1)], 8: [lambda: g_u.pass_z(0)], 9: [lambda: g_g.pass_x(2)],
+        10: [lambda: g_u.pass_z(1)], 13: [lambda: g_u.pass_z(2)], 14: [lambda: g_u.pass_x(3)], 15: [lambda: g_u.pass_x(0)],
+        16: [lambda: g_d.pass_z(0)], 17: [lambda: g_u.pass_x(1)], 19: [lambda: g_d.pass_z(1), lambda: g_u.pass_x(2)],
+        23: [lambda: g_d.pass_z(2)],
+    }
+
+    def step(s, carry):
+        p, t = s // tiles, s % tiles
         cols = row_block(p, 128)
-        kh[0], kh[1] = head_masks(k_ref[:, cols].astype(F32), lane, bias)
-        qp = q_ref[:, cols].astype(F32)
-        qh[0] = jnp.where(lane == 64, 1.0, qp).astype(BF16)
-        qh[1] = jnp.where(lane == 0, 1.0, qp).astype(BF16)
-        vh[0, :, :128], vh[1, :, :128] = head_masks(v_ref[:, cols].astype(F32), lane, 0.0)
-
-        def tile_step(t, carry):
-            rows = row_block(t, tile)
-            total = None
-            cols_out = lse_cols[rows, :]
-            for h in range(2):
-                score = nt(qh[h, rows, :], kh[h])
-                top = jnp.max(score, axis=1, keepdims=True)
-                weight = jnp.exp(score - top).astype(BF16)
-                acc = nn(weight, vh[h])
-                part = acc[:, :128] / acc[:, 128:]
-                total = part if total is None else total + part
-                cols_out = jnp.where(lanes_of(tile) == 2 * p + h, top + jnp.log(acc[:, 128:]), cols_out)
-            mixed_ref[rows, cols] = total.astype(BF16)
-            lse_cols[rows, :] = cols_out
-            return carry
-
-        lax.fori_loop(0, tiles, tile_step, 0)
+        for when, events in hooks.items():
+            @pl.when(s == when)
+            def _():
+                for event in events:
+                    event()
+
+        @pl.when(t == 0)
+        def _():
+            kh[0], kh[1] = head_masks(k_ref[:, cols].astype(F32), lane, bias)
+            qp = q_ref[:, cols].astype(F32)
+            qh[0] = jnp.where(lane == 64, 1.0, qp).astype(BF16)
+            qh[1] = jnp.where(lane == 0, 1.0, qp).astype(BF16)
+            vh[0, :, :128], vh[1, :, :128] = head_masks(v_ref[:, cols].astype(F32), lane, 0.0)
+
+        rows = row_block(t, tile)
+        total = None
+        cols_out = lse_cols[rows, :]
+        for h in range(2):
+            score = nt(qh[h, rows, :], kh[h])
+            top = jnp.max(score, axis=1, keepdims=True)
+            weight = jnp.exp(score - top).astype(BF16)
+            acc = nn(weight, vh[h])
+            part = acc[:, :128] / acc[:, 128:]
+            total = part if total is None else total + part
+            cols_out = jnp.where(lanes_of(tile) == 2 * p + h, top + jnp.log(acc[:, 128:]), cols_out)
+        mixed_ref[rows, cols] = total.astype(BF16)
+        lse_cols[rows, :] = cols_out
         return carry
 
-    lax.fori_loop(0, pairs, pair_step, 0)
+    lax.fori_loop(0, pairs * tiles, step, 0)
+    relay_x(g_d)
+    g_o.end()
 
     def project_out(t, carry):
         rows = row_block(t, tile)
-        hidden_ref[rows, :] = x_ref[rows, :].astype(F32) + nn(mixed_ref[rows, :], wo_ref[...])
+        hidden_ref[rows, :] = x_ref[rows, :].astype(F32) + nn(mixed_ref[rows, :], wo[...].reshape(d, d))
         lse_ref[:, rows] = jnp.transpose(lse_cols[rows, :])
         return carry
 
     lax.fori_loop(0, tiles, project_out, 0)
+    g_g.end()
+    g_u.end()
+    g_d.end()
+    outs = [pltpu.make_async_copy(full, out, out_sems.at[i])
+            for i, (full, out) in enumerate(zip(fulls[1:], (out_q, out_k, out_v, out_o, out_g, out_u, out_d)))]
+    for copy in outs:
+        copy.start()
+    for g in gathers:
+        g.sent()
+    cot_copy.wait()
+    for copy in outs:
+        copy.wait()
 
 
 def permuted_store(target, index, value, block):
@@ -593,23 +769,29 @@
     rows, d = query_weight.shape
     ff = gate_weight.shape[1]
     rows_down = down_weight.shape[0]
-    x = lax.all_to_all(plots, "narrow", 0, 1, tiled=True)[0]
-    cot = lax.all_to_all(cotangent, "narrow", 0, 1, tiled=True)[0]
-    slots = x.shape[0]
+    half = plots.shape[1]
+    slots = 2 * half
     counts = plot_grid[:, 0] * plot_grid[:, 1]
     count = lax.dynamic_slice(counts, (lax.axis_index("narrow"),), (1,))
-    gather = functools.partial(lax.all_gather, axis_name="wide", axis=0, tiled=True)
-    gains = lax.all_gather(jnp.stack([gain_attn, gain_mlp]), "wide", axis=1, tiled=True).astype(F32)
-    wq, wk, wv, wo = gather(query_weight), gather(key_weight), gather(value_weight), gather(out_weight)
-    wg, wu, wd = gather(gate_weight), gather(up_weight), gather(down_weight)
     act = lambda dtype=BF16: ((slots, d), dtype)
     vm = lambda shape, dtype=BF16: pltpu.VMEM(shape, dtype)
-    q, k, v, normed, mixed, lse, hidden = call(
-        attend_forward,
-        [act(), act(), act(), act(), act(), ((128, slots), F32), act(F32)],
-        [vm((2, slots, 128)), vm((2, slots, 128)), vm((2, slots, 256)), vm((slots, 128), F32)],
-        (count, x, gains[0:1], wq, wk, wv, wo),
-    )
+    fulls = [(16, rows, d)] * 4 + [(16, rows, ff)] * 2 + [(16, rows_down, d)]
+    outs = [act(), act(), act(), act(), act(), ((128, slots), F32), act(F32), act(), act(), ((2, d), F32)]
+    outs += [(shape, BF16) for shape in fulls]
+    results = pl.pallas_call(
+        gather_forward,
+        out_shape=[jax.ShapeDtypeStruct(shape, dtype) for shape, dtype in outs],
+        in_specs=[pl.BlockSpec(memory_space=pltpu.SMEM)] + [pl.BlockSpec(memory_space=pltpu.VMEM)] * 11,
+        out_specs=[pl.BlockSpec(memory_space=pltpu.VMEM)] * 10 + [pl.BlockSpec(memory_space=pl.ANY)] * 7,
+        scratch_shapes=[vm((2, slots, 128)), vm((2, slots, 128)), vm((2, slots, 256)), vm((slots, 128), F32)]
+        + [vm(shape) for shape in fulls] + [vm((16, 8, 128), F32)]
+        + [pltpu.SemaphoreType.DMA((8, 15)), pltpu.SemaphoreType.DMA((8, 16)), pltpu.SemaphoreType.DMA((4,)),
+           pltpu.SemaphoreType.DMA((7,))],
+        compiler_params=pltpu.CompilerParams(vmem_limit_bytes=VMEM_BYTES, collective_id=1, has_side_effects=True),
+    )(count, plots, cotangent, gain_attn.reshape(1, -1), gain_mlp.reshape(1, -1), query_weight, key_weight, value_weight,
+      out_weight, gate_weight, up_weight, down_weight)
+    q, k, v, normed, mixed, lse, hidden, x, cot, gains = results[:10]
+    wq, wk, wv, wo, wg, wu, wd = [w.reshape(-1, w.shape[2]) for w in results[10:]]
     output, dhid, g_down, g_gate, g_up, gg_mlp = call(
         mlp_both,
         [act(), act(F32), ((ff, d), BF16), ((d, ff), BF16), ((d, ff), BF16), ((1, d), F32)],

time: 1010 us -> 825 us (0.82)
  waiting for transfers between devices: 625 us -> 398 us
  Pallas kernels: 176 us -> 250 us
  blocking collectives: 82.1 us -> 60.3 us
    all_gather x7 -> x0, waiting for transfers between devices: 202 us -> none  [the longest x3 96.1 us: body_plot(): wg, wu, wd = (gather(gate_weight), gather(up_weight), gather(down_weight))]
    pallas_call x0 -> x1, Pallas kernels: none -> 117 us  [body_plot(): pl.pallas_call(gather_forward, out_shape=[jax.ShapeDtypeStruct(shape, dty...]
    pallas_call x3 -> x2, Pallas kernels: 176 us -> 133 us  [call(): pl.pallas_call(kernel, out_shape=[jax.ShapeDtypeStruct(shape, dtype) for...]
    all_gather x1 -> x0, blocking collectives: 21.7 us -> none  [body_plot(): lax.all_gather(jnp.stack([gain_attn, gain_mlp]), 'wide', axis=1, tiled=True)]
    all_to_all x2 -> x0, waiting for transfers between devices: 20.1 us -> none  [the longest x1 20.1 us: body_plot(): x = lax.all_to_all(plots, 'narrow', 0, 1, tiled=True)[0]]
    unnamed x3 -> x2, other arithmetic: 32.6 us -> 32.6 us
  transfers between devices with their start and end apart: 19 -> 10, of which waited for: 14 -> 7; matrix products, arithmetic and copies ran while one was open for 7% -> 8% of each run, Pallas kernels for 4% -> 0%
where the time goes in v2:
time: 825 us; the launch traced here: 816 us
  waiting for transfers between devices  398 us (48%)
  Pallas kernels  250 us (30%)
  blocking collectives  60.3 us (7%)
  other arithmetic  41.3 us (5%)
  local copies, waits for them, and re-layouts  41.2 us (5%)
  between operations  14.5 us (2%)
  starting transfers between devices  9.69 us (1%)
    reduce_scatter x7, waiting for transfers between devices, reduce(): lax.psum_scatter(unpermute(grad, rows), 'wide', scatter_dimension=0, tile...  398 us
    pallas_call x2, Pallas kernels, call(): pl.pallas_call(kernel, out_shape=[jax.ShapeDtypeStruct(shape, dtype) for...  133 us
    pallas_call x1, Pallas kernels, body_plot(): pl.pallas_call(gather_forward, out_shape=[jax.ShapeDtypeStruct(shape, dty...  117 us
    psum x1, blocking collectives, reduce_gain(): total = lax.psum(grad[0], ('wide', 'narrow'))  60.3 us
    unnamed x2, other arithmetic  32.6 us
    unnamed x29, local copies, waits for them, and re-layouts  17.4 us
  transfers between devices with their start and end apart: 10, of which 7 were waited for; matrix products, arithmetic and copies ran while one was open for 8% of the time, Pallas kernels for 0%

profile of v2, /device:TPU:0, one launch (start us, length us, event | category | flops | bytes accessed | tf_op | source)
XLA Modules:
  0.0 815.7 jit_solution(15825286401112908234)
XLA Ops:
  8.6 116.8 %shard_map.203 = (bf16[1024,768]{1,0:T(8,128)(2,1)}, bf16[1024,768]{1,0:T(8,128)(2,1)}, bf16[1024,768]{1,0:T(8,128)(2,1)}, bf16[1024,768]{1,0:T(8,128)(2,1)}, bf...) custom-call(s32[1]{0:T(128)} %bitcast.count_ref, ...), custom_call_target="tpu_custom_call" | custom-call | tf_op jit(solution)/shard_map/pallas_call | solution.py:781
  126.8 64.9 %shard_map.204 = (bf16[1024,768]{1,0:T(8,128)(2,1)}, f32[1024,768]{1,0:T(8,128)}, bf16[2048,768]{1,0:T(8,128)(2,1)}, bf16[768,2048]{1,0:T(8,128)(2,1)}, bf16[768,2048]{1,0:T(8,128)(2,1)}, /*index=5*/f32[1,768]{1,0:T(1,128)}) custom-call(f32[1024,768]{1,0:T(8,128)} %get-tuple-element.40.hidden_ref, bf16[1024,768]{1,0:T(8,128)(2,1)} %get-tuple-element.41.cot_ref, ...), custom_call_target="tpu_custom_call" | custom-call | tf_op jit(solution)/shard_map/pallas_call | solution.py:751
  191.7 68.5 %shard_map.205 = (bf16[1024,768]{1,0:T(8,128)(2,1)}, bf16[768,768]{1,0:T(8,128)(2,1)}, bf16[768,768]{1,0:T(8,128)(2,1)}, bf16[768,768]{1,0:T(8,128)(2,1)}, bf16[768,768]{1,0:T(8,128)(2,1)}, /*index=5*/f32[1,768]{1,0:T(1,128)}) custom-call(s32[1]{0:T(128)} %bitcast.count_ref, bf16[1024,768]{1,0:T(8,128)(2,1)} %get-tuple-element.47.x_ref, ...), custom_call_target="tpu_custom_call" | custom-call | tf_op jit(solution)/shard_map/pallas_call | solution.py:751
  260.2 2.5 copy.42
  265.8 2.5 copy.41
  268.4 1.9 copy.45
  270.4 1.9 copy-done.1
  272.2 1.9 copy.46
  274.2 1.9 copy-done
  276.1 1.9 copy.47
  278.0 3.9 copy.52
  282.3 21.0 %reduce.3 = bf16[1024,768]{1,0:T(8,128)(2,1)} reduce(bf16[1024,1,768]{2,1,0:T(2,128)(2,1)S(1)} %bitcast.53, bf16[]{:T(256)} %broadcast.2), dimensions={1}, to_apply=%bitcast.48.reduce_sub_computation | reduce | bytes 3145730
  303.3 2.5 reshape.126
  305.8 4.6 all-to-all-start.1
  310.5 9.7 %reduce-scatter.10.cloned.1.call-done = bf16[48,768]{1,0:T(8,128)(2,1)} async-done(((bf16[768,768]{1,0:T(8,128)(2,1)}), bf16[48,768]{1,0:T(8,128)(2,1)}) %reduce-scatter.10.cloned.1.call-update) | async-done | bytes 73744 | tf_op jit(solution)/shard_map/reduce_scatter | solution.py:811
  320.1 60.7 %reduce-scatter.12.cloned.1.call-done = bf16[48,768]{1,0:T(8,128)(2,1)} async-done(((bf16[768,768]{1,0:T(8,128)(2,1)}), bf16[48,768]{1,0:T(8,128)(2,1)}) %reduce-scatter.12.cloned.1.call-update) | async-done | bytes 73744 | tf_op jit(solution)/shard_map/reduce_scatter | solution.py:811
  380.8 60.5 %reduce-scatter.14.cloned.1.call-done = bf16[48,768]{1,0:T(8,128)(2,1)} async-done(((bf16[768,768]{1,0:T(8,128)(2,1)}), bf16[48,768]{1,0:T(8,128)(2,1)}) %reduce-scatter.14.cloned.1.call-update) | async-done | bytes 73744 | tf_op jit(solution)/shard_map/reduce_scatter | solution.py:811
  441.3 60.6 %reduce-scatter.8.cloned.1.call-done = bf16[48,768]{1,0:T(8,128)(2,1)} async-done(((bf16[768,768]{1,0:T(8,128)(2,1)}), bf16[48,768]{1,0:T(8,128)(2,1)}) %reduce-scatter.8.cloned.1.call-update) | async-done | bytes 73744 | tf_op jit(solution)/shard_map/reduce_scatter | solution.py:811
  501.9 69.0 %reduce-scatter.16.cloned.1.call-done = bf16[48,2048]{1,0:T(8,128)(2,1)} async-done(((bf16[768,2048]{1,0:T(8,128)(2,1)}), bf16[48,2048]{1,0:T(8,128)(2,1)}) %reduce-scatter.16.cloned.1.call-update) | async-done | bytes 196624 | tf_op jit(solution)/shard_map/reduce_scatter | solution.py:811
  570.9 68.9 %reduce-scatter.18.cloned.1.call-done = bf16[48,2048]{1,0:T(8,128)(2,1)} async-done(((bf16[768,2048]{1,0:T(8,128)(2,1)}), bf16[48,2048]{1,0:T(8,128)(2,1)}) %reduce-scatter.18.cloned.1.call-update) | async-done | bytes 196624 | tf_op jit(solution)/shard_map/reduce_scatter | solution.py:811
  639.7 69.0 %reduce-scatter.20.cloned.1.call-done = bf16[128,768]{1,0:T(8,128)(2,1)} async-done(((bf16[2048,768]{1,0:T(8,128)(2,1)}), bf16[128,768]{1,0:T(8,128)(2,1)}) %reduce-scatter.20.cloned.1.call-update) | async-done | bytes 196624 | tf_op jit(solution)/shard_map/reduce_scatter | solution.py:811
  708.8 3.8 copy.53
  712.6 11.6 %reduce.2 = bf16[1024,768]{1,0:T(8,128)(2,1)} reduce(bf16[1024,1,768]{2,1,0:T(2,128)(2,1)S(1)} %bitcast.54, bf16[]{:T(256)} %broadcast.2), dimensions={1}, to_apply=%bitcast.49.reduce_sub_computation | reduce | bytes 3145730
  724.2 2.5 reshape.124
  726.7 4.8 all-to-all-start
  731.5 60.3 %all-reduce = (f32[768]{0:T(1024)S(1)}, f32[768]{0:T(1024)S(1)}) all-reduce(f32[768]{0:T(1024)S(1)} %reduce, f32[768]{0:T(1024)S(1)} %reduce.1), channel_id=1, replica_groups=mesh['wide'=16,'narrow'=2] {'wide','narrow'}, use_global_device_ids=true, to_apply=%region_14.0 | all-reduce | flops 1536 | bytes 12288 | tf_op jit(solution)/shard_map/psum | solution.py:815
  793.0 2.5 reshape.127
  796.9 2.5 reshape.125
  799.4 1.4 copy.48
  800.8 1.7 convert_element_type.25
  802.5 1.7 convert_element_type.26
  804.2 1.7 convert_element_type.27
  (54 shorter events, 11.7 us)
Async XLA Ops:
  7.2 312.9 %reduce-scatter.10.cloned.1.call-start = ((), (), s32[]{:S(2)}) async-start(), calls=%async_computation.10 | async-start | bytes 1253376 | tf_op jit(solution)/shard_map/reduce_scatter | solution.py:811
  260.2 2.6 copy-start.4
  262.8 118.0 %reduce-scatter.12.cloned.1.call-start = ((), (), s32[]{:S(2)}) async-start(), calls=%async_computation.11 | async-start | bytes 1253376 | tf_op jit(solution)/shard_map/reduce_scatter | solution.py:811
  262.8 1.7 copy-start.3
  264.0 177.3 %reduce-scatter.14.cloned.1.call-start = ((), (), s32[]{:S(2)}) async-start(), calls=%async_computation.12 | async-start | bytes 1253376 | tf_op jit(solution)/shard_map/reduce_scatter | solution.py:811
  265.7 236.2 %reduce-scatter.8.cloned.1.call-start = ((), (), s32[]{:S(2)}) async-start(), calls=%async_computation.9 | async-start | bytes 1253376 | tf_op jit(solution)/shard_map/reduce_scatter | solution.py:811
  265.7 2.6 copy-start.2
  268.3 302.6 %reduce-scatter.16.cloned.1.call-start = ((), (), s32[]{:S(2)}) async-start(), calls=%async_computation.13 | async-start | bytes 3342336 | tf_op jit(solution)/shard_map/reduce_scatter | solution.py:811
  270.3 1.9 copy-start.1
  270.3 369.4 %reduce-scatter.18.cloned.1.call-start = ((), (), s32[]{:S(2)}) async-start(), calls=%async_computation.14 | async-start | bytes 3342336 | tf_op jit(solution)/shard_map/reduce_scatter | solution.py:811
  274.1 1.9 copy-start
  274.1 434.6 %reduce-scatter.20.cloned.1.call-start = ((), (), s32[]{:S(2)}) async-start(), calls=%async_computation.15 | async-start | bytes 3342336 | tf_op jit(solution)/shard_map/reduce_scatter | solution.py:811
  305.8 420.9 %all-to-all-start.1 = ((bf16[2,2,196608]{2,1,0:T(2,128)(2,1)}), bf16[2,2,196608]{2,1,0:T(2,128)(2,1)}, u32[]{:S(2)}, u32[]{:S(2)}) async-start(bf16[2,2,196608]{2,1,0:T(2,128)(2,1)} %reshape.126), calls=%async_computation.1 | async-start | bytes 3145728 | tf_op jit(solution)/shard_map/all_to_all | solution.py:818
  310.4 490.4 %all-reduce.4.cloned.1.call-start = ((), (), s32[]{:S(2)}) async-start(), calls=%async_computation.16 | async-start | bytes 1769472 | tf_op jit(solution)/shard_map/psum | solution.py:812
  726.7 4.8 copy-start.10
  726.7 4.8 copy-start.9
  726.7 70.2 %all-to-all-start = ((bf16[2,2,196608]{2,1,0:T(2,128)(2,1)}), bf16[2,2,196608]{2,1,0:T(2,128)(2,1)}, u32[]{:S(2)}, u32[]{:S(2)}) async-start(bf16[2,2,196608]{2,1,0:T(2,128)(2,1)} %reshape.124), calls=%async_computation | async-start | bytes 3145728 | tf_op jit(solution)/shard_map/all_to_all | solution.py:818
  800.8 5.2 copy-start.8
  800.8 5.8 copy-start.7
  800.8 6.5 copy-start.6
  800.8 7.2 copy-start.5
Sparse Core Ops, SparseCore 0:
  262.9 57.1 reduce-scatter.9
  323.7 57.0 reduce-scatter.11
  384.4 56.8 reduce-scatter.13
  444.8 57.0 reduce-scatter.7
  505.6 65.2 reduce-scatter.15
  574.6 65.1 reduce-scatter.17
  643.5 65.1 reduce-scatter.19
  711.5 46.4 all-reduce.3

commit v3 on v2

--- a/solution.py
+++ b/solution.py
@@ -578,6 +578,82 @@
         copy.wait()
 
 
+class Scatter:
+    def __init__(self, place, mine, base, theirs, recv_c, recv_x, recv_z, recv_y, out, send, recv):
+        self.place, self.mine, self.base, self.theirs = place, mine, base, theirs
+        self.recv_c, self.recv_x, self.recv_z, self.recv_y, self.out = recv_c, recv_x, recv_z, recv_y, out
+        self.sends, self.recvs = send, recv
+
+    def copy(self, stage, source, target, device):
+        return pltpu.make_async_remote_copy(
+            src_ref=source, dst_ref=target, send_sem=self.sends.at[stage], recv_sem=self.recvs.at[stage],
+            device_id=device, device_id_type=MESH_ID)
+
+    def core_copy(self):
+        return self.copy(0, self.theirs, self.recv_c, self.place.to_core())
+
+    def x_copy(self):
+        p = self.place
+        return self.copy(1, self.mine.at[pl.ds(self.base + (1 - p.x) * 4, 4)], self.recv_x, p.to_x())
+
+    def z_copy(self, j):
+        p = self.place
+        return self.copy(2 + j, self.mine.at[self.base + p.x * 4 + p.other_z(j)], self.recv_z.at[j], p.to_z(j))
+
+    def y_copy(self):
+        p = self.place
+        return self.copy(5, self.mine.at[self.base + p.x * 4 + p.z], self.recv_y, p.to_y())
+
+    def start(self):
+        self.core_copy().start()
+
+    def add_core(self):
+        self.core_copy().wait_recv()
+
+        def step(i, carry):
+            self.mine[self.base + i] = self.mine[self.base + i] + self.recv_c[i]
+            return carry
+
+        lax.fori_loop(0, 8, step, 0)
+
+    def send_x(self):
+        self.x_copy().start()
+
+    def add_x(self):
+        self.x_copy().wait_recv()
+        first = self.base + self.place.x * 4
+
+        def step(i, carry):
+            self.mine[first + i] = self.mine[first + i] + self.recv_x[i]
+            return carry
+
+        lax.fori_loop(0, 4, step, 0)
+        for j in (2, 1, 0):
+            self.z_copy(j).start()
+
+    def add_z(self):
+        for j in range(3):
+            self.z_copy(j).wait_recv()
+        own = self.base + self.place.x * 4 + self.place.z
+        total = self.mine[own].astype(F32)
+        for j in range(3):
+            total = total + self.recv_z[j].astype(F32)
+        self.mine[own] = total.astype(self.mine.dtype)
+        self.y_copy().start()
+
+    def add_y(self):
+        self.y_copy().wait_recv()
+        own = self.base + self.place.x * 4 + self.place.z
+        self.out[...] = self.mine[own].astype(F32) + self.recv_y[...].astype(F32)
+
+    def sent(self):
+        self.core_copy().wait_send()
+        self.x_copy().wait_send()
+        for j in range(3):
+            self.z_copy(j).wait_send()
+        self.y_copy().wait_send()
+
+
 def permuted_store(target, index, value, block):
     blocks = target.shape[0] // block
     deep = blocks // 4
@@ -646,105 +722,210 @@
     lax.fori_loop(0, ff // 256, gate_step, 0)
 
 
-def attend_backward(count_ref, x_ref, gain_ref, wq_ref, wk_ref, wv_ref, wo_ref,
-                    q_ref, k_ref, v_ref, normed_ref, mixed_ref, lse_ref, dhid_ref,
-                    gplots_ref, gq_ref, gk_ref, gv_ref, gout_ref, ggain_ref,
-                    dhl, dmix, dsum, turned, qh, kh, vh, dh, kt, dq_s, dk_s, dv_s, dqt):
-    slots, d = x_ref.shape
+def scatter_backward(count_ref, x_hbm, gains_ref, wq_hbm, wk_hbm, wv_hbm, wo_hbm, q_hbm, k_hbm, v_hbm, mixed_hbm, lse_ref,
+                     dhid_hbm, block_hbm, gdown_hbm, ggate_hbm, gup_hbm, gmlp_ref,
+                     block_out, gplots_out, sum_q, sum_k, sum_v, sum_o, sum_g, sum_u, sum_d, sum_gain,
+                     x_s, wq, wk, wv, wo, q_s, k_s, v_s, mixed_s, dhid_s, dhl, dmix, dsum, mixed_t, normed_t, ggain,
+                     qh, kh, vh, dh, kt, dqt, own_d, own_g, own_u, own_gain, gq, gk, gv, go,
+                     c_d, c_g, c_u, c_q, c_k, c_v, c_o, c_gain, x_d, x_g, x_u, x_q, x_k, x_v, x_o, x_gain,
+                     z_d, z_g, z_u, z_q, z_k, z_v, z_o, z_gain, y_d, y_g, y_u, y_q, y_k, y_v, y_o, y_gain,
+                     sends, recvs, load_sems, out_sems):
+    slots, d = x_s.shape
+    half = slots // 2
     tile = 256
     tiles = slots // tile
     pairs = HEADS // 2
-    blocks = 16
+    rows_own = d // 16
+    place = Place()
+    ours = pl.ds(place.c * 8, 8)
+    pairs_in = ((dhid_hbm, dhid_s), (wo_hbm, wo), (mixed_hbm, mixed_s), (x_hbm, x_s), (gdown_hbm.at[ours], own_d),
+                (ggate_hbm.at[ours], own_g), (gup_hbm.at[ours], own_u), (q_hbm, q_s), (k_hbm, k_s), (v_hbm, v_s),
+                (wq_hbm, wq), (wk_hbm, wk), (wv_hbm, wv))
+    loads = [pltpu.make_async_copy(a, b, load_sems.at[i]) for i, (a, b) in enumerate(pairs_in)]
+    for load in loads:
+        load.start()
+    theirs = pl.ds((1 - place.c) * 8, 8)
+
+    def scatter(i, mine, base, other, c, x, z, y, out):
+        return Scatter(place, mine, base, other, c, x, z, y, out, sends.at[i], recvs.at[i])
+
+    s_d = scatter(0, own_d, 0, gdown_hbm.at[theirs], c_d, x_d, z_d, y_d, sum_d)
+    s_g = scatter(1, own_g, 0, ggate_hbm.at[theirs], c_g, x_g, z_g, y_g, sum_g)
+    s_u = scatter(2, own_u, 0, gup_hbm.at[theirs], c_u, x_u, z_u, y_u, sum_u)
+    base = place.c * 8
+    s_o = scatter(3, go, base, go.at[theirs], c_o, x_o, z_o, y_o, sum_o)
+    s_q = scatter(4, gq, base, gq.at[theirs], c_q, x_q, z_q, y_q, sum_q)
+    s_k = scatter(5, gk, base, gk.at[theirs], c_k, x_k, z_k, y_k, sum_k)
+    s_v = scatter(6, gv, base, gv.at[theirs], c_v, x_v, z_v, y_v, sum_v)
+    s_n = scatter(7, own_gain, base, own_gain.at[theirs], c_gain, x_gain, z_gain, y_gain, sum_gain)
+    mine = pl.ds(pl.multiple_of(place.y * half, half), half)
+    other = pl.ds(pl.multiple_of((1 - place.y) * half, half), half)
+
+    def half_out(source, target, i):
+        far = pltpu.make_async_remote_copy(
+            src_ref=source.at[other], dst_ref=target.at[place.y], send_sem=out_sems.at[3 * i],
+            recv_sem=out_sems.at[3 * i + 1], device_id=place.to_y(), device_id_type=MESH_ID)
+        near = pltpu.make_async_copy(source.at[mine], target.at[place.y], out_sems.at[3 * i + 2])
+        return far, near
+
+    place.greet()
+    block_far, block_near = half_out(block_hbm, block_out, 0)
+    s_d.start()
+    block_far.start()
+    s_g.start()
+    s_u.start()
+    block_near.start()
+
     head_row = lax.broadcasted_iota(jnp.int32, (128, d), 0)
     head_col = lax.broadcasted_iota(jnp.int32, (128, d), 1)
     pick = jnp.where(head_col // HEAD_DIM == head_row, 1.0, 0.0).astype(BF16)
+    for i in range(5):
+        loads[i].wait()
+    s_d.add_core()
+    s_d.send_x()
 
     def first(t, carry):
         rows = row_block(t, tile)
-        low = dhid_ref[rows, :].astype(BF16)
+        low = dhid_s[rows, :].astype(BF16)
         dhl[rows, :] = low
-        grad = nt(low, wo_ref[...]).astype(BF16)
+        grad = nt(low, wo[...].reshape(d, d)).astype(BF16)
         dmix[rows, :] = grad
-        mixed = mixed_ref[rows, :]
+        mixed = mixed_s[rows, :]
         prod = grad.astype(F32) * mixed.astype(F32)
         high = prod.astype(BF16)
         rest = (prod - high.astype(F32)).astype(BF16)
         dsum[:, rows] = nt(pick, high) + nt(pick, rest)
-        permuted_store(turned, rows, mixed, d // blocks)
+        permuted_store(mixed_t, rows, mixed, rows_own)
+        x = x_s[rows, :].astype(F32)
+        r = lax.rsqrt(jnp.mean(x * x, axis=-1, keepdims=True) + epsilon)
+        permuted_store(normed_t, rows, (x * r * gains_ref[0:1, :]).astype(BF16), rows_own)
         return carry
 
     lax.fori_loop(0, tiles, first, 0)
 
-    def weight_grads(target, right):
+    def weight_grads(target, left, right):
         def step(n, carry):
             cols = row_block(n, 256)
-            target[:, cols] = nn(turned[...], right[:, cols]).astype(BF16)
+            target[:, :, cols] = nn(left[...], right[:, cols]).astype(BF16).reshape(16, rows_own, 256)
             return carry
 
         lax.fori_loop(0, d // 256, step, 0)
 
-    weight_grads(gout_ref, dhl)
+    weight_grads(go, mixed_t, dhl)
+    s_o.start()
+    for load in loads[5:]:
+        load.wait()
+    s_g.add_core()
+    s_u.add_core()
+    s_o.add_core()
     count = count_ref[0]
     lane = lanes_of(slots)
     slot = lax.broadcasted_iota(jnp.int32, (slots, 128), 0)
     bias = jnp.where(slot < count, 0.0, -1e30)
-
-    def pair_step(p, carry):
+    hooks = {
+        6: [s_g.send_x], 7: [s_d.add_x], 13: [s_o.send_x], 14: [s_g.add_x], 16: [s_d.add_z, s_u.send_x],
+        17: [s_o.add_x], 19: [s_d.add_y], 22: [s_g.add_z],
+    }
+
+    def step(s, carry):
+        p, t = s // tiles, s % tiles
         cols = row_block(p, 128)
-        kp = k_ref[:, cols].astype(F32)
-        kh[0], kh[1] = head_masks(kp, lane, bias)
+        for when, events in hooks.items():
+            @pl.when(s == when)
+            def _():
+                for event in events:
+                    event()
+
+        @pl.when(t == 0)
+        def _():
+            kp = k_s[:, cols].astype(F32)
+            kh[0], kh[1] = head_masks(kp, lane, bias)
+            for h in range(2):
+                own = (lane < 64) if h == 0 else (lane >= 64)
+                kt[h] = jnp.transpose(jnp.where(own, kp, 0.0)).astype(BF16)
+            qp = q_s[:, cols].astype(F32)
+            qh[0] = jnp.where(lane == 64, 1.0, qp).astype(BF16)
+            qh[1] = jnp.where(lane == 0, 1.0, qp).astype(BF16)
+            qh[2], qh[3] = head_masks(qp, lane, 0.0)
+            vh[0], vh[1] = head_masks(v_s[:, cols].astype(F32), lane, 0.0)
+            dh[0], dh[1] = head_masks(dmix[:, cols].astype(F32), lane, 0.0)
+            dqt[...] = jnp.zeros_like(dqt)
+
+        rows = row_block(t, tile)
+        d_k = d_v = None
         for h in range(2):
-            own = (lane < 64) if h == 0 else (lane >= 64)
-            kt[h] = jnp.transpose(jnp.where(own, kp, 0.0)).astype(BF16)
-        qp = q_ref[:, cols].astype(F32)
-        qh[0] = jnp.where(lane == 64, 1.0, qp).astype(BF16)
-        qh[1] = jnp.where(lane == 0, 1.0, qp).astype(BF16)
-        qh[2], qh[3] = head_masks(qp, lane, 0.0)
-        vh[0], vh[1] = head_masks(v_ref[:, cols].astype(F32), lane, 0.0)
-        grad_pair = dmix[:, cols]
-        dh[0], dh[1] = head_masks(grad_pair.astype(F32), lane, 0.0)
-        dqt[...] = jnp.zeros_like(dqt)
-
-        def tile_step(t, carry):
-            rows = row_block(t, tile)
-            d_k = d_v = None
-            for h in range(2):
-                score = nt(kh[h, rows, :], qh[h])
-                weight = jnp.exp(score - lse_ref[pl.ds(2 * p + h, 1), :])
-                d_att = nt(vh[h, rows, :], dmix[:, cols])
-                d_score = (weight * (d_att - dsum[pl.ds(2 * p + h, 1), :])).astype(BF16)
-                part_v = nn(weight.astype(BF16), dh[h])
-                part_k = nn(d_score, qh[2 + h])
-                d_v = part_v if d_v is None else d_v + part_v
-                d_k = part_k if d_k is None else d_k + part_k
-                dqt[...] += nn(kt[h, :, rows], d_score)
-            dk_s[rows, cols] = d_k.astype(BF16)
-            dv_s[rows, cols] = d_v.astype(BF16)
-            return carry
-
-        lax.fori_loop(0, tiles, tile_step, 0)
-        dq_s[:, cols] = jnp.transpose(dqt[...]).astype(BF16)
+            score = nt(kh[h, rows, :], qh[h])
+            weight = jnp.exp(score - lse_ref[pl.ds(2 * p + h, 1), :])
+            d_att = nt(vh[h, rows, :], dmix[:, cols])
+            d_score = (weight * (d_att - dsum[pl.ds(2 * p + h, 1), :])).astype(BF16)
+            part_v = nn(weight.astype(BF16), dh[h])
+            part_k = nn(d_score, qh[2 + h])
+            d_v = part_v if d_v is None else d_v + part_v
+            d_k = part_k if d_k is None else d_k + part_k
+            dqt[...] += nn(kt[h, :, rows], d_score)
+        k_s[rows, cols] = d_k.astype(BF16)
+        v_s[rows, cols] = d_v.astype(BF16)
+
+        @pl.when(t == tiles - 1)
+        def _():
+            q_s[:, cols] = jnp.transpose(dqt[...]).astype(BF16)
+
         return carry
 
-    lax.fori_loop(0, pairs, pair_step, 0)
-    ggain_ref[...] = jnp.zeros_like(ggain_ref)
-
-    def last(t, carry):
+    lax.fori_loop(0, pairs * tiles, step, 0)
+    for target, right, out in ((gq, q_s, s_q), (gk, k_s, s_k), (gv, v_s, s_v)):
+        weight_grads(target, normed_t, right)
+        out.start()
+    s_u.add_x()
+    for s in (s_q, s_k, s_v):
+        s.add_core()
+        s.send_x()
+    ggain[...] = jnp.zeros_like(ggain)
+    gplots = dhl
+
+    def last(i, carry):
+        t = (i + (tiles // 2) * (1 - place.y)) % tiles
         rows = row_block(t, tile)
-        permuted_store(turned, rows, normed_ref[rows, :], d // blocks)
-        x = x_ref[rows, :].astype(F32)
+        x = x_s[rows, :].astype(F32)
         r = lax.rsqrt(jnp.mean(x * x, axis=-1, keepdims=True) + epsilon)
-        dn = nt(dq_s[rows, :], wq_ref[...]) + nt(dk_s[rows, :], wk_ref[...]) + nt(dv_s[rows, :], wv_ref[...])
-        scaled = dn * gain_ref[...]
+        dn = (nt(q_s[rows, :], wq[...].reshape(d, d)) + nt(k_s[rows, :], wk[...].reshape(d, d))
+              + nt(v_s[rows, :], wv[...].reshape(d, d)))
+        scaled = dn * gains_ref[0:1, :]
         mean = jnp.mean(scaled * x, axis=-1, keepdims=True)
-        gplots_ref[rows, :] = (dhid_ref[rows, :] + r * scaled - x * (r * r * r * mean)).astype(BF16)
-        ggain_ref[...] += jnp.sum(dn * x * r, axis=0, keepdims=True)
+        gplots[rows, :] = (dhid_s[rows, :] + r * scaled - x * (r * r * r * mean)).astype(BF16)
+        ggain[...] += jnp.sum(dn * x * r, axis=0, keepdims=True)
         return carry
 
-    lax.fori_loop(0, tiles, last, 0)
-    weight_grads(gq_ref, dq_s)
-    weight_grads(gk_ref, dk_s)
-    weight_grads(gv_ref, dv_s)
+    gplots_far, gplots_near = half_out(gplots, gplots_out, 1)
+    lax.fori_loop(0, tiles // 2, last, 0)
+    gplots_far.start()
+    s_o.add_z()
+    lax.fori_loop(tiles // 2, tiles, last, 0)
+    gplots_near.start()
+    for w in range(16):
+        z, x, c = w // 4, (w // 2) % 2, w % 2
+        spot = (c * 2 + x) * 4 + z
+        cols = slice(w * rows_own, (w + 1) * rows_own)
+        own_gain[spot, 0:1, 0:rows_own] = ggain[0:1, cols]
+        own_gain[spot, 1:2, 0:rows_own] = gmlp_ref[0:1, cols]
+    s_n.start()
+    s_u.add_z()
+    s_n.add_core()
+    s_n.send_x()
+    for s in (s_q, s_k, s_v, s_n):
+        s.add_x()
+    s_g.add_y()
+    s_o.add_y()
+    for s in (s_q, s_k, s_v, s_n):
+        s.add_z()
+    for s in (s_u, s_q, s_k, s_v, s_n):
+        s.add_y()
+    for s in (s_d, s_g, s_u, s_o, s_q, s_k, s_v, s_n):
+        s.sent()
+    block_far.wait()
+    block_near.wait()
+    gplots_far.wait()
+    gplots_near.wait()
 
 
 def call(kernel, outs, scratch, args, scalars=1):
@@ -757,11 +938,6 @@
         scratch_shapes=scratch,
         compiler_params=pltpu.CompilerParams(vmem_limit_bytes=VMEM_BYTES),
     )(*args)
-
-
-def unpermute(grad, rows):
-    cols = grad.shape[1]
-    return grad.reshape(2, 2, -1, rows, cols).transpose(2, 1, 0, 3, 4).reshape(-1, cols)
 
 
 def body_plot(plots, plot_grid, query_weight, key_weight, value_weight, out_weight, gate_weight, up_weight, down_weight,
@@ -791,33 +967,42 @@
     )(count, plots, cotangent, gain_attn.reshape(1, -1), gain_mlp.reshape(1, -1), query_weight, key_weight, value_weight,
       out_weight, gate_weight, up_weight, down_weight)
     q, k, v, normed, mixed, lse, hidden, x, cot, gains = results[:10]
-    wq, wk, wv, wo, wg, wu, wd = [w.reshape(-1, w.shape[2]) for w in results[10:]]
+    wq, wk, wv, wo = results[10:14]
+    wg, wu, wd = [w.reshape(-1, w.shape[2]) for w in results[14:]]
     output, dhid, g_down, g_gate, g_up, gg_mlp = call(
         mlp_both,
         [act(), act(F32), ((ff, d), BF16), ((d, ff), BF16), ((d, ff), BF16), ((1, d), F32)],
         [vm((d, slots)), vm((ff, slots)), vm((slots, ff)), vm((slots, ff))],
         (hidden, cot, gains[1:2], wg, wu, wd), 0,
     )
-    gplots, g_q, g_k, g_v, g_out, gg_attn = call(
-        attend_backward,
-        [act(), ((d, d), BF16), ((d, d), BF16), ((d, d), BF16), ((d, d), BF16), ((1, d), F32)],
-        [vm((slots, d)), vm((slots, d)), vm((128, slots), F32), vm((d, slots)), vm((4, slots, 128)), vm((2, slots, 128)),
-         vm((2, slots, 128)), vm((2, slots, 128)), vm((2, 128, slots)), vm((slots, d)), vm((slots, d)), vm((slots, d)),
-         vm((128, slots), F32)],
-        (count, x, gains[0:1], wq, wk, wv, wo, q, k, v, normed, mixed, lse, dhid),
-    )
-
-    def reduce(grad, rows):
-        part = lax.psum_scatter(unpermute(grad, rows), "wide", scatter_dimension=0, tiled=True)
-        return lax.psum(part, "narrow").astype(F32)
-
-    def reduce_gain(grad):
-        total = lax.psum(grad[0], ("wide", "narrow"))
-        return lax.dynamic_slice(total, (lax.axis_index("wide") * rows,), (rows,))
-
-    back = lambda value: lax.all_to_all(value[None], "narrow", 1, 0, tiled=True)
-    return (back(output), back(gplots), reduce(g_q, rows), reduce(g_k, rows), reduce(g_v, rows), reduce(g_out, rows),
-            reduce(g_gate, rows), reduce(g_up, rows), reduce(g_down, rows_down), reduce_gain(gg_attn), reduce_gain(gg_mlp))
+    shapes = [(rows_down, d), (rows, ff), (rows, ff), (rows, d), (rows, d), (rows, d), (rows, d)]
+    scatters = shapes + [(8, 128)]
+    dtypes = [BF16] * 7 + [F32]
+    spaces = [pl.BlockSpec(memory_space=pltpu.SMEM), pl.BlockSpec(memory_space=pl.ANY), pl.BlockSpec(memory_space=pltpu.VMEM)]
+    spaces += [pl.BlockSpec(memory_space=pl.ANY)] * 8 + [pl.BlockSpec(memory_space=pltpu.VMEM)]
+    spaces += [pl.BlockSpec(memory_space=pl.ANY)] * 5 + [pl.BlockSpec(memory_space=pltpu.VMEM)]
+    sums = [(rows, d)] * 4 + [(rows, ff)] * 2 + [(rows_down, d), (8, 128)]
+    big = lambda dtype=BF16: pltpu.VMEM((slots, d), dtype)
+    full = lambda: vm((16, rows, d))
+    stages = lambda lead: [vm(lead + shape, dtype) for shape, dtype in zip(scatters, dtypes)]
+    results = pl.pallas_call(
+        scatter_backward,
+        out_shape=[jax.ShapeDtypeStruct(plots.shape, BF16)] * 2 + [jax.ShapeDtypeStruct(shape, F32) for shape in sums],
+        in_specs=spaces,
+        out_specs=[pl.BlockSpec(memory_space=pl.ANY)] * 2 + [pl.BlockSpec(memory_space=pltpu.VMEM)] * 8,
+        scratch_shapes=[big(), full(), full(), full(), full(), big(), big(), big(), big(), big(F32), big(), big(),
+                        vm((128, slots), F32), vm((d, slots)), vm((d, slots)), vm((1, d), F32),
+                        vm((4, slots, 128)), vm((2, slots, 128)), vm((2, slots, 128)), vm((2, slots, 128)),
+                        vm((2, 128, slots)), vm((128, slots), F32),
+                        vm((8, rows_down, d)), vm((8, rows, ff)), vm((8, rows, ff)), vm((16, 8, 128), F32),
+                        full(), full(), full(), full()]
+        + stages((8,)) + stages((4,)) + stages((3,)) + stages(())
+        + [pltpu.SemaphoreType.DMA((8, 6)), pltpu.SemaphoreType.DMA((8, 6)), pltpu.SemaphoreType.DMA((13,)),
+           pltpu.SemaphoreType.DMA((6,))],
+        compiler_params=pltpu.CompilerParams(vmem_limit_bytes=VMEM_BYTES, collective_id=2, has_side_effects=True),
+    )(count, x, gains, wq, wk, wv, wo, q, k, v, mixed, lse, dhid, output, g_down.reshape(16, rows_down, d),
+      g_gate.reshape(16, rows, ff), g_up.reshape(16, rows, ff), gg_mlp)
+    return (*results[:9], results[9][0, :rows], results[9][1, :rows])
 
 
 def body_for(mesh):

time: 825 us -> 309 us (0.37); the launches traced: 816 us -> 309 us
  waiting for transfers between devices: 398 us -> 0 us
  blocking collectives: 60.3 us -> 0 us
  Pallas kernels: 250 us -> 295 us
  other arithmetic: 41.3 us -> 0.83 us
  local copies, waits for them, and re-layouts: 41.2 us -> 11.9 us
  between operations: 14.5 us -> 0.7 us
  starting transfers between devices: 9.69 us -> 0 us
    reduce_scatter x7 -> x0, waiting for transfers between devices: 398 us -> none  [reduce(): lax.psum_scatter(unpermute(grad, rows), 'wide', scatter_dimension=0, tile...]
    pallas_call x0 -> x1, Pallas kernels: none -> 113 us  [body_plot(): pl.pallas_call(scatter_backward, out_shape=[jax.ShapeDtypeStruct(plots.sh...]
    pallas_call x2 -> x1, Pallas kernels: 133 us -> 64.9 us  [call(): pl.pallas_call(kernel, out_shape=[jax.ShapeDtypeStruct(shape, dtype) for...]
    psum x1 -> x0, blocking collectives: 60.3 us -> none  [reduce_gain(): total = lax.psum(grad[0], ('wide', 'narrow'))]
    unnamed x2 -> x0, other arithmetic: 32.6 us -> none
    transpose x7 -> x0, local copies, waits for them, and re-layouts: 13 us -> none  [unpermute(): grad.reshape(2, 2, -1, rows, cols).transpose(2, 1, 0, 3, 4)]
    all_to_all x2 -> x0, starting transfers between devices: 9.36 us -> none  [body_plot(): back = lambda value: lax.all_to_all(value[None], 'narrow', 1, 0, tiled=True)]
    unnamed x29 -> x25, local copies, waits for them, and re-layouts: 17.4 us -> 8.83 us
  transfers between devices with their start and end apart: 10 -> 0, of which waited for: 7 -> 0; matrix products, arithmetic and copies ran while one was open for 8% -> 0% of each run, Pallas kernels for 0% -> 0%
where the time goes in v3:
time: 309 us
  Pallas kernels  295 us (95%)
  local copies, waits for them, and re-layouts  11.9 us (4%)
    pallas_call x1, Pallas kernels, body_plot(): pl.pallas_call(gather_forward, out_shape=[jax.ShapeDtypeStruct(shape, dty...  117 us
    pallas_call x1, Pallas kernels, body_plot(): pl.pallas_call(scatter_backward, out_shape=[jax.ShapeDtypeStruct(plots.sh...  113 us
    pallas_call x1, Pallas kernels, call(): pl.pallas_call(kernel, out_shape=[jax.ShapeDtypeStruct(shape, dtype) for...  64.9 us
    unnamed x25, local copies, waits for them, and re-layouts  8.83 us

profile of v3, /device:TPU:0, one launch (start us, length us, event | category | flops | bytes accessed | tf_op | source)
XLA Modules:
  0.0 308.8 jit_solution(11203264105497286165)
XLA Ops:
  0.6 0.8 slice_multiply_fusion
  1.5 0.5 constant_dynamic-slice_fusion
  2.0 117.0 %shard_map.203 = (bf16[1024,768]{1,0:T(8,128)(2,1)}, bf16[1024,768]{1,0:T(8,128)(2,1)}, bf16[1024,768]{1,0:T(8,128)(2,1)}, bf16[1024,768]{1,0:T(8,128)(2,1)}, bf...) custom-call(s32[1]{0:T(128)} %bitcast.count_ref, ...), custom_call_target="tpu_custom_call" | custom-call | tf_op jit(solution)/shard_map/pallas_call | solution.py:957
  119.0 1.3 slice.17.gain_ref
  120.3 64.9 %shard_map.204 = (bf16[1024,768]{1,0:T(8,128)(2,1)}, f32[1024,768]{1,0:T(8,128)}, bf16[2048,768]{1,0:T(8,128)(2,1)}, bf16[768,2048]{1,0:T(8,128)(2,1)}, bf16[768,2048]{1,0:T(8,128)(2,1)}, /*index=5*/f32[1,768]{1,0:T(1,128)}) custom-call(f32[1024,768]{1,0:T(8,128)} %get-tuple-element.54.hidden_ref, bf16[1024,768]{1,0:T(8,128)(2,1)} %get-tuple-element.55.cot_ref, ...), custom_call_target="tpu_custom_call" | custom-call | tf_op jit(solution)/shard_map/pallas_call | solution.py:932
  185.2 113.4 %shard_map.205 = (bf16[2,512,768]{2,1,0:T(8,128)(2,1)}, bf16[2,512,768]{2,1,0:T(8,128)(2,1)}, f32[48,768]{1,0:T(8,128)}, f32[48,768]{1,0:T(8,128)}, f32[48,768]{...) custom-call(s32[1]{0:T(128)} %bitcast.count_ref, ...), custom_call_target="tpu_custom_call" | custom-call | tf_op jit(solution)/shard_map/pallas_call | solution.py:988
  298.6 1.3 slice_bitcast_fusion
  299.9 0.0 copy-start
  299.9 2.8 copy.32
  302.7 0.0 copy-done
  302.7 0.0 copy-start.7
  302.7 0.0 copy-start.6
  302.7 0.0 copy-start.5
  302.7 0.0 copy-start.4
  302.7 0.0 copy-start.3
  302.7 1.1 copy.33
  303.9 0.0 copy-done.7
  303.9 0.0 copy-start.2
  303.9 0.0 copy-start.1
  303.9 0.7 copy.34
  304.5 0.0 copy-done.6
  304.5 0.7 copy.35
  305.2 0.0 copy-done.5
  305.2 0.7 copy.36
  305.9 0.0 copy-done.4
  305.9 0.7 copy.37
  306.5 0.0 copy-done.3
  306.5 0.7 copy.38
  307.3 0.0 copy-done.2
  307.3 0.7 copy.39
  308.0 0.0 copy-done.1
  308.0 0.7 copy.40
Async XLA Ops:
  299.9 2.8 copy-start
  302.7 1.2 copy-start.7
  302.7 1.8 copy-start.6
  302.7 2.5 copy-start.5
  302.7 3.2 %copy-start.4 = (f32[48,768]{1,0:T(8,128)S(1)}, f32[48,768]{1,0:T(8,128)}, u32[]{:S(2)}) copy-start(f32[48,768]{1,0:T(8,128)} %get-tuple-element.93) | copy-start | bytes 442372
  302.7 3.8 %copy-start.3 = (f32[48,2048]{1,0:T(8,128)S(1)}, f32[48,2048]{1,0:T(8,128)}, u32[]{:S(2)}) copy-start(f32[48,2048]{1,0:T(8,128)} %get-tuple-element.94) | copy-start | bytes 1179652
  303.9 3.4 %copy-start.2 = (f32[48,2048]{1,0:T(8,128)S(1)}, f32[48,2048]{1,0:T(8,128)}, u32[]{:S(2)}) copy-start(f32[48,2048]{1,0:T(8,128)} %get-tuple-element.95) | copy-start | bytes 1179652
  303.9 4.2 %copy-start.1 = (f32[128,768]{1,0:T(8,128)S(1)}, f32[128,768]{1,0:T(8,128)}, u32[]{:S(2)}) copy-start(f32[128,768]{1,0:T(8,128)} %get-tuple-element.96) | copy-start | bytes 1179652
